TPU v7x, 32 devices: a whole 2x2x4 slice. The times are simulated.
32 devices in a mesh: sec: 2 (over core), row: 4 (over y, x), nest: 4 (over z).
Axes of the slice: x: 2, y: 2, z: 4, core: 2. Of those that a mesh axis runs over, the one named last changes fastest.
Arguments:
- ocean_state: float32 [2, 3, 256, 512], P('sec', None, 'row', 'nest'), may hold values from -1.2 to 1.2
- face_depth: float32 [2, 2, 256, 512], P('sec', None, 'row', 'nest'), may hold values from 2 to 4
- face_open: int32 [2, 2, 256, 512], P('sec', None, 'row', 'nest'), may hold values 0 or 1
- nest_place: int32 [16], replicated, may hold values from 0 to 95, as said below
- nest_host: int32 [16], replicated, may hold values from 0 to 31, as said below
Outputs:
- final_state: float32 [2, 3, 256, 512], P('sec', None, 'row', 'nest')
Inputs may be any that keep to these rules, and one draw needn't show every extreme that they name: `nest_place`: distinct positions; the first and the last position are always covered. `nest_host`: distinct slots; both slots of some device hold a nest; the nest at the first position lives in the last slot and the nest at the last position in the first slot.
All inputs are finite; a program needn't handle non-finite values. No bound on the sum of `face_open` on one device may be relied on, other than what follows from the above.
Results may differ from a plain program's by a relative error of at most 0.00013.
Values sent between devices are 32-bit elements; how exact they have to be, the bound alone decides.
A program may use at most 64 MiB of HBM per device.

v0:
```python
import jax
import jax.numpy as jnp
from jax import lax
from jax.sharding import PartitionSpec as P

PH = 8
PW = 32
RR = 4
K = 2
STEPS = 4


COURANT = 0.3
HIGHEST = lax.Precision.HIGHEST


def padded_2(shard, sides, width):
    for axis, dim in sides:
        size, length = (lax.axis_size(axis), shard.shape[dim])
        up = [(i, (i + 1) % size) for i in range(size - 1)]
        down = [(j, i) for i, j in up]
        last = lax.slice_in_dim(shard, length - width, length, axis=dim)
        leading = lax.slice_in_dim(shard, 0, width, axis=dim)
        before = lax.ppermute(last, axis, up)
        after = lax.ppermute(leading, axis, down)
        shard = jnp.concatenate([before, shard, after], axis=dim)
    return shard


def surface_update(surface, eastward, southward, west_ghost, north_ghost):
    east_behind = jnp.concatenate([west_ghost, eastward[..., :-1]], axis=-1)
    south_behind = jnp.concatenate([north_ghost, southward[..., :-1, :]], axis=-2)
    return surface - COURANT * (eastward - east_behind + (southward - south_behind))


def flux_update(
    eastward,
    southward,
    new_surface,
    surface_east,
    surface_south,
    depth_east,
    depth_south,
    open_east,
    open_south,
):
    new_eastward = open_east * (
        eastward
        - COURANT * (depth_east + 0.5 * (new_surface + surface_east)) * (surface_east - new_surface)
    )
    new_southward = open_south * (
        southward
        - COURANT
        * (depth_south + 0.5 * (new_surface + surface_south))
        * (surface_south - new_surface)
    )
    return (new_eastward, new_southward)


def restrict(surface, eastward, southward):
    leading = surface.shape[:-2]
    coarse_surface = surface.reshape(leading + (PH, RR, PW, RR)).mean(axis=(-3, -1))
    coarse_east = eastward[..., RR - 1 :: RR].reshape(leading + (PH, RR, PW)).mean(axis=-2)
    coarse_south = southward[..., RR - 1 :: RR, :].reshape(leading + (PH, PW, RR)).mean(axis=-1)
    return jnp.stack([coarse_surface, coarse_east, coarse_south], axis=-3)


def cycle_strips(tile_state):
    tile_cols = tile_state.shape[2]
    top_rows = (RR - 1) * PH // 2
    left_cols = PW // 2
    span_cols = (RR - 1) * PW
    banded = tile_state.reshape(3, K, RR * PH, tile_cols)
    rows_mid = banded[:, :, top_rows : top_rows + PH, :]
    west_flux = rows_mid[1, :, :, left_cols - 1 : left_cols - 1 + span_cols : PW]
    east_level = rows_mid[0, :, :, left_cols + PW : left_cols + PW + span_cols : PW]
    north_flux = banded[2, :, top_rows - 1, left_cols : left_cols + span_cols].reshape(
        K, RR - 1, PW
    )
    south_level = banded[0, :, top_rows + PH, left_cols : left_cols + span_cols].reshape(
        K, RR - 1, PW
    )
    first_row = jnp.concatenate([west_flux.transpose(0, 2, 1), north_flux], axis=-1)
    second = jnp.concatenate([east_level.transpose(0, 2, 1), south_level], axis=-1)
    return jnp.stack([first_row, second], axis=2).reshape(K * (RR - 1), 2, PH + PW)


def apply_feedback(tile_state, feedback, covered):
    tile_rows = tile_state.shape[1]
    tile_cols = tile_state.shape[2]
    top_rows = (RR - 1) * PH // 2
    left_cols = PW // 2
    span_cols = (RR - 1) * PW
    banded = tile_state.reshape(3, K, RR * PH, tile_cols)
    feedback_block = (
        feedback.reshape(K, RR - 1, 3, PH, PW).transpose(2, 0, 3, 1, 4).reshape(3, K, PH, span_cols)
    )
    covered_mask = jnp.repeat(covered.reshape(K, RR - 1), PW, axis=1)[None, :, None, :]
    middle = banded[:, :, top_rows : top_rows + PH, left_cols : left_cols + span_cols]
    banded = banded.at[:, :, top_rows : top_rows + PH, left_cols : left_cols + span_cols].set(
        jnp.where(covered_mask, feedback_block, middle)
    )
    return banded.reshape(3, tile_rows, tile_cols)


def outer_update(padded, depth_tile, open_tile, last_row, last_col):
    surface, eastward, southward = (padded[0], padded[1], padded[2])
    extended = surface[1:, 1:] - COURANT * (
        eastward[1:, 1:] - eastward[1:, :-1] + (southward[1:, 1:] - southward[:-1, 1:])
    )
    tile_rows = extended.shape[0] - 1
    tile_cols = extended.shape[1] - 1
    new_surface = extended[:tile_rows, :tile_cols]
    east_ghost = extended[:tile_rows, tile_cols:] * jnp.where(last_col, 0.0, 1.0)
    south_ghost = extended[tile_rows:, :tile_cols] * jnp.where(last_row, 0.0, 1.0)
    surface_east = jnp.concatenate([new_surface[:, 1:], east_ghost], axis=1)
    surface_south = jnp.concatenate([new_surface[1:, :], south_ghost], axis=0)
    new_eastward, new_southward = flux_update(
        eastward[1 : tile_rows + 1, 1 : tile_cols + 1],
        southward[1 : tile_rows + 1, 1 : tile_cols + 1],
        new_surface,
        surface_east,
        surface_south,
        depth_tile[0],
        depth_tile[1],
        open_tile[0],
        open_tile[1],
    )
    return jnp.stack([new_surface, new_eastward, new_southward])


def nest_update(tile_state, depth_tile, open_tile, slot_live, old_strips, new_strips):
    tile_rows = tile_state.shape[1]
    tile_cols = tile_state.shape[2]
    fine_rows = tile_rows // K
    fine = tile_state.reshape(3, K, fine_rows, tile_cols)
    depth_fine = depth_tile.reshape(2, K, fine_rows, tile_cols)
    open_fine = open_tile.reshape(2, K, fine_rows, tile_cols)
    surface, eastward, southward = (fine[0], fine[1], fine[2])
    live_mask = slot_live[:, None, None]
    for substep in range(1, RR + 1):
        ghost_vals = old_strips + substep / RR * (new_strips - old_strips)
        west_ghost = jnp.repeat(ghost_vals[:, 0, :PH], RR, axis=1)[:, :, None]
        north_ghost = jnp.repeat(ghost_vals[:, 0, PH:], RR, axis=1)[:, None, :]
        east_ghost = jnp.repeat(ghost_vals[:, 1, :PH], RR, axis=1)[:, :, None]
        south_ghost = jnp.repeat(ghost_vals[:, 1, PH:], RR, axis=1)[:, None, :]
        new_surface = surface_update(surface, eastward, southward, west_ghost, north_ghost)
        surface_east = jnp.concatenate([new_surface[..., 1:], east_ghost], axis=-1)
        surface_south = jnp.concatenate([new_surface[..., 1:, :], south_ghost], axis=-2)
        new_eastward, new_southward = flux_update(
            eastward,
            southward,
            new_surface,
            surface_east,
            surface_south,
            depth_fine[0],
            depth_fine[1],
            open_fine[0],
            open_fine[1],
        )
        surface = jnp.where(live_mask, new_surface, surface)
        eastward = jnp.where(live_mask, new_eastward, eastward)
        southward = jnp.where(live_mask, new_southward, southward)
    return jnp.stack([surface, eastward, southward]).reshape(3, tile_rows, tile_cols)


def route_strips(tile_state, is_outer, selector, slot_count):

    def build_strips(carried):
        return jnp.einsum("gp,pcx->gcx", selector, cycle_strips(carried), precision=HIGHEST)

    def silent_strips(carried):
        return jnp.zeros((slot_count, 2, PH + PW), jnp.float32)

    outgoing = lax.cond(is_outer, build_strips, silent_strips, tile_state)
    widened = jnp.concatenate([jnp.zeros_like(outgoing), outgoing], axis=0)
    incoming = lax.all_to_all(
        widened, ("sec", "row", "nest"), split_axis=0, concat_axis=0, tiled=True
    )
    return incoming.reshape(-1, K, 2, PH + PW).sum(axis=0)


def route_returns(tile_state, is_outer, slot_live, slot_target, tile_count):
    target_count = lax.axis_size("sec") * tile_count

    def build_returns(carried):
        fine = carried.reshape(3, K, carried.shape[1] // K, carried.shape[2])
        coarse = restrict(fine[0], fine[1], fine[2])
        onehot = (
            (jnp.arange(target_count, dtype=jnp.int32)[:, None] == slot_target[None, :])
            & slot_live[None, :]
        ).astype(jnp.float32)
        return (onehot[:, :, None, None, None] * coarse[None]).reshape(target_count * K, 3, PH, PW)

    def silent_returns(carried):
        return jnp.zeros((target_count * K, 3, PH, PW), jnp.float32)

    outgoing = lax.cond(is_outer, silent_returns, build_returns, tile_state)
    incoming = lax.all_to_all(
        outgoing, ("sec", "row", "nest"), split_axis=0, concat_axis=0, tiled=True
    )
    incoming = incoming[incoming.shape[0] - tile_count * K :]
    return incoming


def on_device(ocean_state, face_depth, face_open, nest_place, nest_host):
    tile_state = ocean_state[0]
    depth_tile = face_depth[0]
    open_tile = face_open[0].astype(jnp.float32)
    row_count = lax.axis_size("row")
    col_count = lax.axis_size("nest")
    tile_count = row_count * col_count
    slot_count = tile_count * K
    position_count = K * (RR - 1)
    tile_index = lax.axis_index("row") * col_count + lax.axis_index("nest")
    is_outer = lax.axis_index("sec") == 0
    last_row = lax.axis_index("row") == row_count - 1
    last_col = lax.axis_index("nest") == col_count - 1
    host_hot = (nest_host[:, None] == jnp.arange(slot_count, dtype=jnp.int32)[None, :]).astype(
        jnp.float32
    )
    matches = (
        nest_place[:, None]
        == tile_index * position_count + jnp.arange(position_count, dtype=jnp.int32)[None, :]
    ).astype(jnp.float32)
    selector = jnp.dot(host_hot.T, matches, precision=HIGHEST)
    covered = jnp.sum(selector, axis=0) > 0.5
    my_slots = nest_host[:, None] == tile_index * K + jnp.arange(K, dtype=jnp.int32)[None, :]
    slot_live = jnp.any(my_slots, axis=0)
    slot_target = jnp.sum(jnp.where(my_slots, (nest_place // position_count)[:, None], 0), axis=0)

    def advance_outer(padded, carried):
        return outer_update(padded, depth_tile, open_tile, last_row, last_col)

    def hold_outer(padded, carried):
        return carried

    def hold_nests(carried, old_strips, new_strips):
        return carried

    def advance_nests(carried, old_strips, new_strips):
        return nest_update(carried, depth_tile, open_tile, slot_live, old_strips, new_strips)

    def merge_returns(carried, incoming):
        feedback = jnp.einsum("gp,gcxy->pcxy", selector, incoming, precision=HIGHEST)
        return apply_feedback(carried, feedback, covered)

    def hold_returns(carried, incoming):
        return carried

    old_strips = route_strips(tile_state, is_outer, selector, slot_count)
    for timestep in range(STEPS):
        padded = padded_2(tile_state, (("row", 1), ("nest", 2)), 1)
        tile_state = lax.cond(is_outer, advance_outer, hold_outer, padded, tile_state)
        new_strips = route_strips(tile_state, is_outer, selector, slot_count)
        tile_state = lax.cond(
            is_outer, hold_nests, advance_nests, tile_state, old_strips, new_strips
        )
        incoming = route_returns(tile_state, is_outer, slot_live, slot_target, tile_count)
        tile_state = lax.cond(is_outer, merge_returns, hold_returns, tile_state, incoming)
        old_strips = new_strips
    return tile_state[None]


def solution(mesh):
    placed = (
        P("sec", None, "row", "nest"),
        P("sec", None, "row", "nest"),
        P("sec", None, "row", "nest"),
        P(),
        P(),
    )
    return jax.shard_map(
        on_device,
        mesh=mesh,
        in_specs=placed,
        out_specs=P("sec", None, "row", "nest"),
        check_vma=False,
    )
```

profile of v0, /device:TPU:0, one launch (start us, length us, event | category | flops | bytes accessed | tf_op | source)
XLA Modules:
  0.0 229.5 jit_solution(2492326327378202569)
XLA Ops:
  0.0 0.9 copy.898
  0.9 4.9 %collective-permute-start = (f32[3,1,128]{2,1,0:T(1,128)S(1)}, f32[3,1,128]{2,1,0:T(1,128)S(1)}, u32[]{:S(2)}, u32[]{:S(2)}) collective-permute-start(f32[3,1,128]{2,1,0:T(1,128)S(1)} %get-tuple-element.810), channel_id=1, source_target_pairs={{0,4},{4,8},{8,12},{1,5},{5,9},{9,13},{2,6},{6,10},{10,14},{3,7},{... | collective-permute-start | bytes 4616 | tf_op jit(solution)/shard_map/ppermute | solution.py:24
  5.8 1.3 collective-permute-start.1
  8.1 0.9 conditional.23
  9.8 7.0 %all-to-all-start.1 = ((f32[32,1,160]{2,1,0:T(1,128)}), f32[32,1,160]{2,1,0:T(1,128)S(1)}, u32[]{:S(2)}, u32[]{:S(2)}) async-start(f32[32,1,160]{2,1,0:T(1,128)} %reshape.2193), calls=%async_computation.1 | async-start | bytes 65536 | tf_op jit(solution)/shard_map/all_to_all | solution.py:177
  17.0 3.7 %collective-permute-start.2 = (f32[3,66,1]{2,1,0:T(8,128)S(1)}, f32[3,66,1]{2,1,0:T(8,128)S(1)}, u32[]{:S(2)}, u32[]{:S(2)}) collective-permute-start(f32[3,66,1]{2,1,0:T(8,128)S(1)} %get-tuple-element.802), channel_id=1, source_target_pairs={{0,1},{1,2},{2,3},{4,5},{5,6},{6,7},{8,9},{9,10},{10,11},{12,13},{... | collective-permute-start | bytes 2384 | tf_op jit(solution)/shard_map/ppermute | solution.py:24
  20.7 1.3 collective-permute-start.3
  22.2 1.1 collective-permute-done.2
  23.3 4.1 %collective-permute-done.3 = f32[3,66,1]{2,1,0:T(8,128)S(1)} collective-permute-done((f32[3,66,1]{2,1,0:T(8,128)S(1)}, f32[3,66,1]{2,1,0:T(8,128)S(1)}, u32[]{:S(2)}, u32[]{:S(2)}) %collective-permute-start.3) | collective-permute-done | bytes 824 | tf_op jit(solution)/shard_map/ppermute | solution.py:25
  28.0 0.9 conditional.22
  29.0 0.8 reshape.2191
  29.8 4.6 %all-to-all-start = ((f32[32,1,160]{2,1,0:T(1,128)}), f32[32,1,160]{2,1,0:T(1,128)S(1)}, u32[]{:S(2)}, u32[]{:S(2)}) async-start(f32[32,1,160]{2,1,0:T(1,128)} %reshape.2191), calls=%async_computation | async-start | bytes 65536 | tf_op jit(solution)/shard_map/all_to_all | solution.py:177
  35.9 5.7 %all-to-all-done = f32[32,1,160]{2,1,0:T(1,128)S(1)} async-done(((f32[32,1,160]{2,1,0:T(1,128)}), f32[32,1,160]{2,1,0:T(1,128)S(1)}, u32[]{:S(2)}, u32[]{:S(2)}) %all-to-all-start) | async-done | bytes 20512 | tf_op jit(solution)/shard_map/all_to_all | solution.py:177
  42.6 1.0 reshape.2195
  43.6 9.3 %all-to-all-start.2 = ((f32[32,1,1536]{2,1,0:T(1,128)}), f32[32,1,1536]{2,1,0:T(1,128)S(1)}, u32[]{:S(2)}, u32[]{:S(2)}) async-start(f32[32,1,1536]{2,1,0:T(1,128)} %reshape.2195), calls=%async_computation.2 | async-start | bytes 393216 | tf_op jit(solution)/shard_map/all_to_all | solution.py:199
  52.9 9.4 %all-to-all-done.2 = f32[32,1,1536]{2,1,0:T(1,128)S(1)} async-done(((f32[32,1,1536]{2,1,0:T(1,128)}), f32[32,1,1536]{2,1,0:T(1,128)S(1)}, u32[]{:S(2)}, u32[]{:S(2)}) %all-to-all-start.2) | async-done | bytes 196640 | tf_op jit(solution)/shard_map/all_to_all | solution.py:199
  62.3 1.1 reduce.50
  63.6 3.1 %conditional.26 = (f32[3,64,128]{2,1,0:T(8,128)S(1)}) conditional(s32[]{:T(128)} %convert_element_type.59, f32[3,64,128]{2,1,0:T(8,128)S(1)} %get-tuple-element.823, (f32[3,64,128]{2,1,0:T(8,128)S(1)}, pred[6]{0:T(512)(128)(4,1)S(1)}, f32[32,6]{0,1:T(8,128)S(1)}, f32[64,3,8,32]{3,2,1,0:T(8,128)S(1)}) %tuple.157), branch_computations={%region_18.19_spmd, %region_19.20_spmd} | conditional | flops 1774080 | bytes 1012510 | solution.py:260
  64.5 2.1 scatter.6
  66.7 2.8 %collective-permute-start.4 = (f32[3,1,128]{2,1,0:T(1,128)S(1)}, f32[3,1,128]{2,1,0:T(1,128)S(1)}, u32[]{:S(2)}, u32[]{:S(2)}) collective-permute-start(f32[3,1,128]{2,1,0:T(1,128)S(1)} %get-tuple-element.808), channel_id=1, source_target_pairs={{0,4},{4,8},{8,12},{1,5},{5,9},{9,13},{2,6},{6,10},{10,14},{3,7},{... | collective-permute-start | bytes 4616 | tf_op jit(solution)/shard_map/ppermute | solution.py:24
  69.5 1.3 collective-permute-start.5
  70.8 4.2 %collective-permute-done.5 = f32[3,1,128]{2,1,0:T(1,128)S(1)} collective-permute-done((f32[3,1,128]{2,1,0:T(1,128)S(1)}, f32[3,1,128]{2,1,0:T(1,128)S(1)}, u32[]{:S(2)}, u32[]{:S(2)}) %collective-permute-start.5) | collective-permute-done | bytes 1568 | tf_op jit(solution)/shard_map/ppermute | solution.py:25
  75.0 2.3 %collective-permute-start.6 = (f32[3,66,1]{2,1,0:T(8,128)S(1)}, f32[3,66,1]{2,1,0:T(8,128)S(1)}, u32[]{:S(2)}, u32[]{:S(2)}) collective-permute-start(f32[3,66,1]{2,1,0:T(8,128)S(1)} %get-tuple-element.800), channel_id=1, source_target_pairs={{0,1},{1,2},{2,3},{4,5},{5,6},{6,7},{8,9},{9,10},{10,11},{12,13},{... | collective-permute-start | bytes 2384 | tf_op jit(solution)/shard_map/ppermute | solution.py:24
  77.4 1.3 collective-permute-start.7
  78.7 1.0 collective-permute-done.6
  79.7 4.3 %collective-permute-done.7 = f32[3,66,1]{2,1,0:T(8,128)S(1)} collective-permute-done((f32[3,66,1]{2,1,0:T(8,128)S(1)}, f32[3,66,1]{2,1,0:T(8,128)S(1)}, u32[]{:S(2)}, u32[]{:S(2)}) %collective-permute-start.7) | collective-permute-done | bytes 824 | tf_op jit(solution)/shard_map/ppermute | solution.py:25
  84.6 0.9 conditional.28
  85.6 0.8 reshape.2197
  86.4 3.0 %all-to-all-start.3 = ((f32[32,1,160]{2,1,0:T(1,128)}), f32[32,1,160]{2,1,0:T(1,128)S(1)}, u32[]{:S(2)}, u32[]{:S(2)}) async-start(f32[32,1,160]{2,1,0:T(1,128)} %reshape.2197), calls=%async_computation.3 | async-start | bytes 65536 | tf_op jit(solution)/shard_map/all_to_all | solution.py:177
  89.3 7.2 %all-to-all-done.3 = f32[32,1,160]{2,1,0:T(1,128)S(1)} async-done(((f32[32,1,160]{2,1,0:T(1,128)}), f32[32,1,160]{2,1,0:T(1,128)S(1)}, u32[]{:S(2)}, u32[]{:S(2)}) %all-to-all-start.3) | async-done | bytes 20512 | tf_op jit(solution)/shard_map/all_to_all | solution.py:177
  98.0 18.4 %all_to_all.45 = f32[32,1,1536]{2,1,0:T(1,128)S(1)} all-to-all(f32[32,1,1536]{2,1,0:T(1,128)S(1)} %reshape.2199), channel_id=1, replica_groups=mesh['sec'=2,'row'=4,'nest'=4] {'sec','row','nest'}, dimensions={0} | all-to-all | bytes 393216 | tf_op jit(solution)/shard_map/all_to_all | solution.py:199
  116.4 1.1 reduce.52
  117.7 3.1 %conditional.31 = (f32[3,64,128]{2,1,0:T(8,128)S(1)}) conditional(s32[]{:T(128)} %convert_element_type.59, f32[3,64,128]{2,1,0:T(8,128)S(1)} %get-tuple-element.828, (f32[3,64,128]{2,1,0:T(8,128)S(1)}, pred[6]{0:T(512)(128)(4,1)S(1)}, f32[32,6]{0,1:T(8,128)S(1)}, f32[64,3,8,32]{3,2,1,0:T(8,128)S(1)}) %tuple.164), branch_computations={%region_32.33_spmd, %region_33.34_spmd} | conditional | flops 1774080 | bytes 1012510 | solution.py:260
  118.7 2.1 scatter.10
  120.8 2.8 %collective-permute-start.8 = (f32[3,1,128]{2,1,0:T(1,128)S(1)}, f32[3,1,128]{2,1,0:T(1,128)S(1)}, u32[]{:S(2)}, u32[]{:S(2)}) collective-permute-start(f32[3,1,128]{2,1,0:T(1,128)S(1)} %get-tuple-element.806), channel_id=1, source_target_pairs={{0,4},{4,8},{8,12},{1,5},{5,9},{9,13},{2,6},{6,10},{10,14},{3,7},{... | collective-permute-start | bytes 4616 | tf_op jit(solution)/shard_map/ppermute | solution.py:24
  123.6 1.3 collective-permute-start.9
  124.9 4.2 %collective-permute-done.9 = f32[3,1,128]{2,1,0:T(1,128)S(1)} collective-permute-done((f32[3,1,128]{2,1,0:T(1,128)S(1)}, f32[3,1,128]{2,1,0:T(1,128)S(1)}, u32[]{:S(2)}, u32[]{:S(2)}) %collective-permute-start.9) | collective-permute-done | bytes 1568 | tf_op jit(solution)/shard_map/ppermute | solution.py:25
  129.2 2.3 %collective-permute-start.10 = (f32[3,66,1]{2,1,0:T(8,128)S(1)}, f32[3,66,1]{2,1,0:T(8,128)S(1)}, u32[]{:S(2)}, u32[]{:S(2)}) collective-permute-start(f32[3,66,1]{2,1,0:T(8,128)S(1)} %get-tuple-element.798), channel_id=1, source_target_pairs={{0,1},{1,2},{2,3},{4,5},{5,6},{6,7},{8,9},{9,10},{10,11},{12,13},{... | collective-permute-start | bytes 2384 | tf_op jit(solution)/shard_map/ppermute | solution.py:24
  131.5 1.3 collective-permute-start.11
  132.8 1.0 collective-permute-done.10
  133.8 4.3 %collective-permute-done.11 = f32[3,66,1]{2,1,0:T(8,128)S(1)} collective-permute-done((f32[3,66,1]{2,1,0:T(8,128)S(1)}, f32[3,66,1]{2,1,0:T(8,128)S(1)}, u32[]{:S(2)}, u32[]{:S(2)}) %collective-permute-start.11) | collective-permute-done | bytes 824 | tf_op jit(solution)/shard_map/ppermute | solution.py:25
  138.8 0.9 conditional.33
  139.8 0.8 reshape.2201
  140.5 3.0 %all-to-all-start.5 = ((f32[32,1,160]{2,1,0:T(1,128)}), f32[32,1,160]{2,1,0:T(1,128)S(1)}, u32[]{:S(2)}, u32[]{:S(2)}) async-start(f32[32,1,160]{2,1,0:T(1,128)} %reshape.2201), calls=%async_computation.5 | async-start | bytes 65536 | tf_op jit(solution)/shard_map/all_to_all | solution.py:177
  143.5 7.2 %all-to-all-done.5 = f32[32,1,160]{2,1,0:T(1,128)S(1)} async-done(((f32[32,1,160]{2,1,0:T(1,128)}), f32[32,1,160]{2,1,0:T(1,128)S(1)}, u32[]{:S(2)}, u32[]{:S(2)}) %all-to-all-start.5) | async-done | bytes 20512 | tf_op jit(solution)/shard_map/all_to_all | solution.py:177
  152.0 18.4 %all_to_all.46 = f32[32,1,1536]{2,1,0:T(1,128)S(1)} all-to-all(f32[32,1,1536]{2,1,0:T(1,128)S(1)} %reshape.2203), channel_id=1, replica_groups=mesh['sec'=2,'row'=4,'nest'=4] {'sec','row','nest'}, dimensions={0} | all-to-all | bytes 393216 | tf_op jit(solution)/shard_map/all_to_all | solution.py:199
  170.4 1.1 reduce.54
  171.7 3.1 %conditional.36 = (f32[3,64,128]{2,1,0:T(8,128)S(1)}) conditional(s32[]{:T(128)} %convert_element_type.59, f32[3,64,128]{2,1,0:T(8,128)S(1)} %get-tuple-element.833, (f32[3,64,128]{2,1,0:T(8,128)S(1)}, pred[6]{0:T(512)(128)(4,1)S(1)}, f32[32,6]{0,1:T(8,128)S(1)}, f32[64,3,8,32]{3,2,1,0:T(8,128)S(1)}) %tuple.171), branch_computations={%region_46.47_spmd, %region_47.48_spmd} | conditional | flops 1774080 | bytes 1012510 | solution.py:260
  172.6 2.1 scatter.12
  174.8 2.8 %collective-permute-start.12 = (f32[3,1,128]{2,1,0:T(1,128)S(1)}, f32[3,1,128]{2,1,0:T(1,128)S(1)}, u32[]{:S(2)}, u32[]{:S(2)}) collective-permute-start(f32[3,1,128]{2,1,0:T(1,128)S(1)} %get-tuple-element.804), channel_id=1, source_target_pairs={{0,4},{4,8},{8,12},{1,5},{5,9},{9,13},{2,6},{6,10},{10,14},{3,7},{... | collective-permute-start | bytes 4616 | tf_op jit(solution)/shard_map/ppermute | solution.py:24
  177.6 1.3 collective-permute-start.13
  178.9 4.2 %collective-permute-done.13 = f32[3,1,128]{2,1,0:T(1,128)S(1)} collective-permute-done((f32[3,1,128]{2,1,0:T(1,128)S(1)}, f32[3,1,128]{2,1,0:T(1,128)S(1)}, u32[]{:S(2)}, u32[]{:S(2)}) %collective-permute-start.13) | collective-permute-done | bytes 1568 | tf_op jit(solution)/shard_map/ppermute | solution.py:25
  183.2 2.3 %collective-permute-start.14 = (f32[3,66,1]{2,1,0:T(8,128)S(1)}, f32[3,66,1]{2,1,0:T(8,128)S(1)}, u32[]{:S(2)}, u32[]{:S(2)}) collective-permute-start(f32[3,66,1]{2,1,0:T(8,128)S(1)} %get-tuple-element.796), channel_id=1, source_target_pairs={{0,1},{1,2},{2,3},{4,5},{5,6},{6,7},{8,9},{9,10},{10,11},{12,13},{... | collective-permute-start | bytes 2384 | tf_op jit(solution)/shard_map/ppermute | solution.py:24
  185.5 1.3 collective-permute-start.15
  186.8 1.0 collective-permute-done.14
  187.8 4.3 %collective-permute-done.15 = f32[3,66,1]{2,1,0:T(8,128)S(1)} collective-permute-done((f32[3,66,1]{2,1,0:T(8,128)S(1)}, f32[3,66,1]{2,1,0:T(8,128)S(1)}, u32[]{:S(2)}, u32[]{:S(2)}) %collective-permute-start.15) | collective-permute-done | bytes 824 | tf_op jit(solution)/shard_map/ppermute | solution.py:25
  192.8 0.9 conditional.38
  193.7 0.8 reshape.2205
  194.5 3.2 %all-to-all-start.7 = ((f32[32,1,160]{2,1,0:T(1,128)}), f32[32,1,160]{2,1,0:T(1,128)S(1)}, u32[]{:S(2)}, u32[]{:S(2)}) async-start(f32[32,1,160]{2,1,0:T(1,128)} %reshape.2205), calls=%async_computation.7 | async-start | bytes 65536 | tf_op jit(solution)/shard_map/all_to_all | solution.py:177
  197.7 7.0 %all-to-all-done.7 = f32[32,1,160]{2,1,0:T(1,128)S(1)} async-done(((f32[32,1,160]{2,1,0:T(1,128)}), f32[32,1,160]{2,1,0:T(1,128)S(1)}, u32[]{:S(2)}, u32[]{:S(2)}) %all-to-all-start.7) | async-done | bytes 20512 | tf_op jit(solution)/shard_map/all_to_all | solution.py:177
  205.9 18.5 %all_to_all.47 = f32[32,1,1536]{2,1,0:T(1,128)S(1)} all-to-all(f32[32,1,1536]{2,1,0:T(1,128)S(1)} %reshape.2207), channel_id=1, replica_groups=mesh['sec'=2,'row'=4,'nest'=4] {'sec','row','nest'}, dimensions={0} | all-to-all | bytes 393216 | tf_op jit(solution)/shard_map/all_to_all | solution.py:199
  224.5 1.1 reduce.56
  225.8 3.1 %conditional.41 = (f32[1,3,64,128]{3,2,1,0:T(8,128)S(1)}) conditional(s32[]{:T(128)} %convert_element_type.59, f32[3,64,128]{2,1,0:T(8,128)S(1)} %get-tuple-element.838, (f32[3,64,128]{2,1,0:T(8,128)S(1)}, pred[6]{0:T(512)(128)(4,1)S(1)}, f32[64,3,8,32]{3,2,1,0:T(8,128)S(1)}, f32[32,6]{0,1:T(8,128)S(1)}) %tuple.404), branch_computations={%region_60.61_spmd, %region_61.62_spmd} | conditional | flops 1774080 | bytes 1012510 | solution.py:260
  226.7 2.1 scatter.13
  (221 shorter events, 22.7 us)
Async XLA Ops:
  0.9 16.0 %collective-permute-start = (f32[3,1,128]{2,1,0:T(1,128)S(1)}, f32[3,1,128]{2,1,0:T(1,128)S(1)}, u32[]{:S(2)}, u32[]{:S(2)}) collective-permute-start(f32[3,1,128]{2,1,0:T(1,128)S(1)} %get-tuple-element.810), channel_id=1, source_target_pairs={{0,4},{4,8},{8,12},{1,5},{5,9},{9,13},{2,6},{6,10},{10,14},{3,7},{... | collective-permute-start | bytes 4616 | tf_op jit(solution)/shard_map/ppermute | solution.py:24
  5.8 11.1 %collective-permute-start.1 = (f32[3,1,128]{2,1,0:T(1,128)S(1)}, f32[3,1,128]{2,1,0:T(1,128)S(1)}, u32[]{:S(2)}, u32[]{:S(2)}) collective-permute-start(f32[3,1,128]{2,1,0:T(1,128)S(1)} %get-tuple-element.811), channel_id=1, source_target_pairs={{4,0},{8,4},{12,8},{5,1},{9,5},{13,9},{6,2},{10,6},{14,10},{7,3},{... | collective-permute-start | bytes 4616 | tf_op jit(solution)/shard_map/ppermute | solution.py:25
  7.1 0.7 copy-start.3
  7.1 0.7 copy-start.4
  9.1 7.8 %copy-start.2 = (s32[1,2,64,128]{3,2,1,0:T(8,128)S(1)}, s32[1,2,64,128]{3,2,1,0:T(8,128)}, u32[]{:S(2)}) copy-start(s32[1,2,64,128]{3,2,1,0:T(8,128)} %param.57) | copy-start | bytes 196612
  9.8 19.9 %all-to-all-start.1 = ((f32[32,1,160]{2,1,0:T(1,128)}), f32[32,1,160]{2,1,0:T(1,128)S(1)}, u32[]{:S(2)}, u32[]{:S(2)}) async-start(f32[32,1,160]{2,1,0:T(1,128)} %reshape.2193), calls=%async_computation.1 | async-start | bytes 65536 | tf_op jit(solution)/shard_map/all_to_all | solution.py:177
  17.0 6.3 %collective-permute-start.2 = (f32[3,66,1]{2,1,0:T(8,128)S(1)}, f32[3,66,1]{2,1,0:T(8,128)S(1)}, u32[]{:S(2)}, u32[]{:S(2)}) collective-permute-start(f32[3,66,1]{2,1,0:T(8,128)S(1)} %get-tuple-element.802), channel_id=1, source_target_pairs={{0,1},{1,2},{2,3},{4,5},{5,6},{6,7},{8,9},{9,10},{10,11},{12,13},{... | collective-permute-start | bytes 2384 | tf_op jit(solution)/shard_map/ppermute | solution.py:24
  20.7 6.7 %collective-permute-start.3 = (f32[3,66,1]{2,1,0:T(8,128)S(1)}, f32[3,66,1]{2,1,0:T(8,128)S(1)}, u32[]{:S(2)}, u32[]{:S(2)}) collective-permute-start(f32[3,66,1]{2,1,0:T(8,128)S(1)} %get-tuple-element.803), channel_id=1, source_target_pairs={{1,0},{2,1},{3,2},{5,4},{6,5},{7,6},{9,8},{10,9},{11,10},{13,12},{... | collective-permute-start | bytes 2384 | tf_op jit(solution)/shard_map/ppermute | solution.py:25
  22.2 5.4 %copy-start.1 = (f32[1,2,64,128]{3,2,1,0:T(8,128)S(1)}, f32[1,2,64,128]{3,2,1,0:T(8,128)}, u32[]{:S(2)}) copy-start(f32[1,2,64,128]{3,2,1,0:T(8,128)} %param.56) | copy-start | bytes 196612
  29.8 11.9 %all-to-all-start = ((f32[32,1,160]{2,1,0:T(1,128)}), f32[32,1,160]{2,1,0:T(1,128)S(1)}, u32[]{:S(2)}, u32[]{:S(2)}) async-start(f32[32,1,160]{2,1,0:T(1,128)} %reshape.2191), calls=%async_computation | async-start | bytes 65536 | tf_op jit(solution)/shard_map/all_to_all | solution.py:177
  43.6 18.6 %all-to-all-start.2 = ((f32[32,1,1536]{2,1,0:T(1,128)}), f32[32,1,1536]{2,1,0:T(1,128)S(1)}, u32[]{:S(2)}, u32[]{:S(2)}) async-start(f32[32,1,1536]{2,1,0:T(1,128)} %reshape.2195), calls=%async_computation.2 | async-start | bytes 393216 | tf_op jit(solution)/shard_map/all_to_all | solution.py:199
  66.7 4.1 %collective-permute-start.4 = (f32[3,1,128]{2,1,0:T(1,128)S(1)}, f32[3,1,128]{2,1,0:T(1,128)S(1)}, u32[]{:S(2)}, u32[]{:S(2)}) collective-permute-start(f32[3,1,128]{2,1,0:T(1,128)S(1)} %get-tuple-element.808), channel_id=1, source_target_pairs={{0,4},{4,8},{8,12},{1,5},{5,9},{9,13},{2,6},{6,10},{10,14},{3,7},{... | collective-permute-start | bytes 4616 | tf_op jit(solution)/shard_map/ppermute | solution.py:24
  69.5 5.5 %collective-permute-start.5 = (f32[3,1,128]{2,1,0:T(1,128)S(1)}, f32[3,1,128]{2,1,0:T(1,128)S(1)}, u32[]{:S(2)}, u32[]{:S(2)}) collective-permute-start(f32[3,1,128]{2,1,0:T(1,128)S(1)} %get-tuple-element.809), channel_id=1, source_target_pairs={{4,0},{8,4},{12,8},{5,1},{9,5},{13,9},{6,2},{10,6},{14,10},{7,3},{... | collective-permute-start | bytes 4616 | tf_op jit(solution)/shard_map/ppermute | solution.py:25
  75.0 4.6 %collective-permute-start.6 = (f32[3,66,1]{2,1,0:T(8,128)S(1)}, f32[3,66,1]{2,1,0:T(8,128)S(1)}, u32[]{:S(2)}, u32[]{:S(2)}) collective-permute-start(f32[3,66,1]{2,1,0:T(8,128)S(1)} %get-tuple-element.800), channel_id=1, source_target_pairs={{0,1},{1,2},{2,3},{4,5},{5,6},{6,7},{8,9},{9,10},{10,11},{12,13},{... | collective-permute-start | bytes 2384 | tf_op jit(solution)/shard_map/ppermute | solution.py:24
  77.4 6.6 %collective-permute-start.7 = (f32[3,66,1]{2,1,0:T(8,128)S(1)}, f32[3,66,1]{2,1,0:T(8,128)S(1)}, u32[]{:S(2)}, u32[]{:S(2)}) collective-permute-start(f32[3,66,1]{2,1,0:T(8,128)S(1)} %get-tuple-element.801), channel_id=1, source_target_pairs={{1,0},{2,1},{3,2},{5,4},{6,5},{7,6},{9,8},{10,9},{11,10},{13,12},{... | collective-permute-start | bytes 2384 | tf_op jit(solution)/shard_map/ppermute | solution.py:25
  86.4 10.2 %all-to-all-start.3 = ((f32[32,1,160]{2,1,0:T(1,128)}), f32[32,1,160]{2,1,0:T(1,128)S(1)}, u32[]{:S(2)}, u32[]{:S(2)}) async-start(f32[32,1,160]{2,1,0:T(1,128)} %reshape.2197), calls=%async_computation.3 | async-start | bytes 65536 | tf_op jit(solution)/shard_map/all_to_all | solution.py:177
  120.8 4.1 %collective-permute-start.8 = (f32[3,1,128]{2,1,0:T(1,128)S(1)}, f32[3,1,128]{2,1,0:T(1,128)S(1)}, u32[]{:S(2)}, u32[]{:S(2)}) collective-permute-start(f32[3,1,128]{2,1,0:T(1,128)S(1)} %get-tuple-element.806), channel_id=1, source_target_pairs={{0,4},{4,8},{8,12},{1,5},{5,9},{9,13},{2,6},{6,10},{10,14},{3,7},{... | collective-permute-start | bytes 4616 | tf_op jit(solution)/shard_map/ppermute | solution.py:24
  123.6 5.5 %collective-permute-start.9 = (f32[3,1,128]{2,1,0:T(1,128)S(1)}, f32[3,1,128]{2,1,0:T(1,128)S(1)}, u32[]{:S(2)}, u32[]{:S(2)}) collective-permute-start(f32[3,1,128]{2,1,0:T(1,128)S(1)} %get-tuple-element.807), channel_id=1, source_target_pairs={{4,0},{8,4},{12,8},{5,1},{9,5},{13,9},{6,2},{10,6},{14,10},{7,3},{... | collective-permute-start | bytes 4616 | tf_op jit(solution)/shard_map/ppermute | solution.py:25
  129.2 4.6 %collective-permute-start.10 = (f32[3,66,1]{2,1,0:T(8,128)S(1)}, f32[3,66,1]{2,1,0:T(8,128)S(1)}, u32[]{:S(2)}, u32[]{:S(2)}) collective-permute-start(f32[3,66,1]{2,1,0:T(8,128)S(1)} %get-tuple-element.798), channel_id=1, source_target_pairs={{0,1},{1,2},{2,3},{4,5},{5,6},{6,7},{8,9},{9,10},{10,11},{12,13},{... | collective-permute-start | bytes 2384 | tf_op jit(solution)/shard_map/ppermute | solution.py:24
  131.5 6.6 %collective-permute-start.11 = (f32[3,66,1]{2,1,0:T(8,128)S(1)}, f32[3,66,1]{2,1,0:T(8,128)S(1)}, u32[]{:S(2)}, u32[]{:S(2)}) collective-permute-start(f32[3,66,1]{2,1,0:T(8,128)S(1)} %get-tuple-element.799), channel_id=1, source_target_pairs={{1,0},{2,1},{3,2},{5,4},{6,5},{7,6},{9,8},{10,9},{11,10},{13,12},{... | collective-permute-start | bytes 2384 | tf_op jit(solution)/shard_map/ppermute | solution.py:25
  140.5 10.2 %all-to-all-start.5 = ((f32[32,1,160]{2,1,0:T(1,128)}), f32[32,1,160]{2,1,0:T(1,128)S(1)}, u32[]{:S(2)}, u32[]{:S(2)}) async-start(f32[32,1,160]{2,1,0:T(1,128)} %reshape.2201), calls=%async_computation.5 | async-start | bytes 65536 | tf_op jit(solution)/shard_map/all_to_all | solution.py:177
  174.8 4.1 %collective-permute-start.12 = (f32[3,1,128]{2,1,0:T(1,128)S(1)}, f32[3,1,128]{2,1,0:T(1,128)S(1)}, u32[]{:S(2)}, u32[]{:S(2)}) collective-permute-start(f32[3,1,128]{2,1,0:T(1,128)S(1)} %get-tuple-element.804), channel_id=1, source_target_pairs={{0,4},{4,8},{8,12},{1,5},{5,9},{9,13},{2,6},{6,10},{10,14},{3,7},{... | collective-permute-start | bytes 4616 | tf_op jit(solution)/shard_map/ppermute | solution.py:24
  177.6 5.5 %collective-permute-start.13 = (f32[3,1,128]{2,1,0:T(1,128)S(1)}, f32[3,1,128]{2,1,0:T(1,128)S(1)}, u32[]{:S(2)}, u32[]{:S(2)}) collective-permute-start(f32[3,1,128]{2,1,0:T(1,128)S(1)} %get-tuple-element.805), channel_id=1, source_target_pairs={{4,0},{8,4},{12,8},{5,1},{9,5},{13,9},{6,2},{10,6},{14,10},{7,3},{... | collective-permute-start | bytes 4616 | tf_op jit(solution)/shard_map/ppermute | solution.py:25
  183.2 4.6 %collective-permute-start.14 = (f32[3,66,1]{2,1,0:T(8,128)S(1)}, f32[3,66,1]{2,1,0:T(8,128)S(1)}, u32[]{:S(2)}, u32[]{:S(2)}) collective-permute-start(f32[3,66,1]{2,1,0:T(8,128)S(1)} %get-tuple-element.796), channel_id=1, source_target_pairs={{0,1},{1,2},{2,3},{4,5},{5,6},{6,7},{8,9},{9,10},{10,11},{12,13},{... | collective-permute-start | bytes 2384 | tf_op jit(solution)/shard_map/ppermute | solution.py:24
  185.5 6.6 %collective-permute-start.15 = (f32[3,66,1]{2,1,0:T(8,128)S(1)}, f32[3,66,1]{2,1,0:T(8,128)S(1)}, u32[]{:S(2)}, u32[]{:S(2)}) collective-permute-start(f32[3,66,1]{2,1,0:T(8,128)S(1)} %get-tuple-element.797), channel_id=1, source_target_pairs={{1,0},{2,1},{3,2},{5,4},{6,5},{7,6},{9,8},{10,9},{11,10},{13,12},{... | collective-permute-start | bytes 2384 | tf_op jit(solution)/shard_map/ppermute | solution.py:25
  194.5 10.2 %all-to-all-start.7 = ((f32[32,1,160]{2,1,0:T(1,128)}), f32[32,1,160]{2,1,0:T(1,128)S(1)}, u32[]{:S(2)}, u32[]{:S(2)}) async-start(f32[32,1,160]{2,1,0:T(1,128)} %reshape.2205), calls=%async_computation.7 | async-start | bytes 65536 | tf_op jit(solution)/shard_map/all_to_all | solution.py:177
  228.9 0.6 copy-start
where the time goes:
time: 230 us; the launch traced here: 229 us
  waiting for transfers between devices  70.2 us (31%)
  starting transfers between devices  64.2 us (28%)
  blocking collectives  55.3 us (24%)
  local copies, waits for them, and re-layouts  24.8 us (11%)
  other arithmetic  10.4 us (5%)
  matrix products  2.83 us (1%)
    all_to_all x3, blocking collectives, route_returns(): lax.all_to_all(outgoing, ('sec', 'row', 'nest'), split_axis=0, concat_axi...  55.3 us
    ppermute x8, waiting for transfers between devices, padded_2(): after = lax.ppermute(leading, axis, down)  29.6 us
    all_to_all x5, waiting for transfers between devices, route_strips(): lax.all_to_all(widened, ('sec', 'row', 'nest'), split_axis=0, concat_axis...  27.1 us
    ppermute x8, starting transfers between devices, padded_2(): before = lax.ppermute(last, axis, up)  23.9 us
    all_to_all x5, starting transfers between devices, route_strips(): lax.all_to_all(widened, ('sec', 'row', 'nest'), split_axis=0, concat_axis...  20.7 us
    ppermute x8, starting transfers between devices, padded_2(): after = lax.ppermute(leading, axis, down)  10.3 us
    unnamed x29, local copies, waits for them, and re-layouts  9.51 us
    all_to_all x1, waiting for transfers between devices, route_returns(): lax.all_to_all(outgoing, ('sec', 'row', 'nest'), split_axis=0, concat_axi...  9.37 us
  transfers between devices with their start and end apart: 22, of which 16 were waited for; matrix products, arithmetic and copies ran while one was open for 3% of the time, Pallas kernels for 0%

commit v1 on v0

v1 whole, which is shorter than its diff:
```python
import functools

import jax
import jax.numpy as jnp
from jax import lax
from jax.experimental import pallas as pl
from jax.experimental.pallas import tpu as pltpu
from jax.sharding import PartitionSpec as P

PH = 8
PW = 32
RR = 4
K = 2
STEPS = 4
NPOS = K * (RR - 1)
COURANT = 0.3
HIGHEST = lax.Precision.HIGHEST
MESH = pl.DeviceIdType.MESH
FINE_ROWS = RR * PH
TOP = (RR - 1) * PH // 2
LEFT = PW // 2


def iota(shape, dim):
    return lax.broadcasted_iota(jnp.int32, shape, dim)


def new_level(surface, eastward, southward, west_ghost, north_ghost):
    rows, cols = iota(surface.shape, 0), iota(surface.shape, 1)
    east_behind = jnp.where(cols == 0, west_ghost, pltpu.roll(eastward, 1, 1))
    south_behind = jnp.where(rows == 0, north_ghost, pltpu.roll(southward, 1, 0))
    return surface - COURANT * ((eastward - east_behind) + (southward - south_behind))


def new_fluxes(eastward, southward, level, east_ghost, south_ghost, depth, opened):
    height, width = level.shape
    rows, cols = iota(level.shape, 0), iota(level.shape, 1)
    level_east = jnp.where(cols == width - 1, east_ghost, pltpu.roll(level, width - 1, 1))
    level_south = jnp.where(rows == height - 1, south_ghost, pltpu.roll(level, height - 1, 0))
    east = opened[0] * (
        eastward - COURANT * (depth[0] + 0.5 * (level + level_east)) * (level_east - level)
    )
    south = opened[1] * (
        southward - COURANT * (depth[1] + 0.5 * (level + level_south)) * (level_south - level)
    )
    return east, south


def dot(a, b):
    return jnp.dot(a, b, precision=HIGHEST, preferred_element_type=jnp.float32)


def pack_strips(tmp):
    width = tmp.shape[2]
    lane, sub = iota((PH, width), 1), iota((PH, width), 0)
    block = jnp.zeros((PH, width), jnp.float32)
    span = (RR - 1) * PW
    inner = (lane >= LEFT) & (lane < LEFT + span)
    for band in range(K):
        first = band * FINE_ROWS + TOP
        east8 = tmp[1, first : first + PH, :]
        level8 = tmp[0, first : first + PH, :]
        for j in range(RR - 1):
            column = LEFT + j * PW
            west_lane = band * 2 * (RR - 1) + j
            east_lane = west_lane + RR - 1
            block = jnp.where(
                lane == west_lane, pltpu.roll(east8, (west_lane - column + 1) % width, 1), block
            )
            block = jnp.where(
                lane == east_lane, pltpu.roll(level8, (east_lane - column - PW) % width, 1), block
            )
        block = jnp.where(inner & (sub == 2 * band), tmp[2, first - 1 : first, :], block)
        block = jnp.where(inner & (sub == 2 * band + 1), tmp[0, first + PH : first + PH + 1, :], block)
    return block


def kernel(
    n_row,
    n_nest,
    place_ref,
    host_ref,
    state_ref,
    depth_ref,
    open_ref,
    out_ref,
    st,
    tmp,
    strips_out,
    strips_in,
    ret_out,
    ret_in,
    east_out,
    south_out,
    level_out,
    west_in,
    north_in,
    east_in,
    south_in,
    spread,
    ghosts,
    strips_now,
    ret_now,
    strip_send,
    strip_recv,
    ret_send,
    ret_recv,
    halo_send,
    halo_recv,
):
    tiles = n_row * n_nest
    nests = place_ref.shape[0]
    sec, row, col = lax.axis_index("sec"), lax.axis_index("row"), lax.axis_index("nest")
    tile = row * n_nest + col
    is_outer = sec == 0
    has_west, has_east = col > 0, col < n_nest - 1
    has_north, has_south = row > 0, row < n_row - 1
    west, east = (sec, row, col - 1), (sec, row, col + 1)
    north, south = (sec, row - 1, col), (sec, row + 1, col)
    links = ((has_west, west), (has_east, east), (has_north, north), (has_south, south))
    height, width = state_ref.shape[2], state_ref.shape[3]

    barrier = pltpu.get_barrier_semaphore()

    @pl.loop(0, tiles)
    def _(i):
        t = lax.rem(tile + i, tiles)
        pl.semaphore_signal(
            barrier, inc=1, device_id=(1 - sec, t // n_nest, lax.rem(t, n_nest)), device_id_type=MESH
        )

    def send_all(src, dst_of, send_sem, recv_sem):
        @pl.loop(0, tiles)
        def _(i):
            t = lax.rem(tile + i + 1, tiles)
            pltpu.make_async_remote_copy(
                src_ref=src,
                dst_ref=dst_of,
                send_sem=send_sem,
                recv_sem=recv_sem,
                device_id=(1 - sec, t // n_nest, lax.rem(t, n_nest)),
                device_id_type=MESH,
            ).start()

    def wait_all(whole, sem):
        pltpu.make_async_copy(whole, whole, sem).wait()

    @pl.when(is_outer)
    def _():
        for present, device in links:

            @pl.when(present)
            def _():
                pl.semaphore_signal(barrier, inc=1, device_id=device, device_id_type=MESH)

        st[...] = state_ref[0]
        depth = [depth_ref[0, i] for i in range(2)]
        opened = [open_ref[0, i].astype(jnp.float32) for i in range(2)]
        slots, covers = [], []
        for p in range(NPOS):
            slot, cover = jnp.int32(0), jnp.int32(0)
            for n in range(nests):
                hit = place_ref[n] == tile * NPOS + p
                slot = jnp.where(hit, host_ref[n], slot)
                cover = jnp.where(hit, 1, cover)
            slots.append(slot)
            covers.append(cover)
        zero_block = jnp.zeros((height, width), jnp.float32)
        for present, buffer in (
            (has_west, west_in),
            (has_east, east_in),
            (has_north, north_in),
            (has_south, south_in),
        ):

            @pl.when(jnp.logical_not(present))
            def _():
                for s in range(STEPS):
                    buffer[s] = jnp.zeros(buffer.shape[1:], jnp.float32)

        peers = jnp.int32(tiles)
        for present, _device in links:
            peers = peers + jnp.where(present, 1, 0)
        pl.semaphore_wait(barrier, peers)

        strips_out[0] = pack_strips(st)
        send_all(strips_out.at[0], strips_in.at[0, tile], strip_send.at[0], strip_recv.at[0])

        def halo(s, kind, src, dst, device):
            return pltpu.make_async_remote_copy(
                src_ref=src,
                dst_ref=dst,
                send_sem=halo_send.at[s, kind],
                recv_sem=halo_recv.at[s, kind],
                device_id=device,
                device_id_type=MESH,
            )

        @pl.loop(0, STEPS)
        def _(s):
            surface, eastward, southward = st[0], st[1], st[2]
            level = new_level(surface, eastward, southward, 0.0, 0.0)
            fluxes = new_fluxes(eastward, southward, level, 0.0, 0.0, depth, opened)
            tmp[0] = level
            tmp[1] = fluxes[0]
            tmp[2] = fluxes[1]
            strips_out[s + 1] = pack_strips(tmp)
            send_all(
                strips_out.at[s + 1],
                strips_in.at[s + 1, tile],
                strip_send.at[s + 1],
                strip_recv.at[s + 1],
            )

            east_out[s] = eastward
            south_out[s] = southward[height - 8 :]
            to_east = halo(s, 0, east_out.at[s], west_in.at[s], east)
            to_south = halo(s, 1, south_out.at[s], north_in.at[s], south)
            to_west = halo(s, 2, level_out.at[s], east_in.at[s], west)
            to_north = halo(s, 3, level_out.at[s, pl.ds(0, 8)], south_in.at[s], north)

            @pl.when(has_east)
            def _():
                to_east.start()

            @pl.when(has_south)
            def _():
                to_south.start()

            @pl.when(has_west)
            def _():
                to_east.wait_recv()

            @pl.when(has_north)
            def _():
                to_south.wait_recv()

            level = new_level(
                surface,
                eastward,
                southward,
                west_in[s][:, width - 1 : width],
                north_in[s][7:8, :],
            )
            level_out[s] = level

            @pl.when(has_west)
            def _():
                to_west.start()

            @pl.when(has_north)
            def _():
                to_north.start()

            @pl.when(has_east)
            def _():
                to_west.wait_recv()

            @pl.when(has_south)
            def _():
                to_north.wait_recv()

            fluxes = new_fluxes(
                eastward, southward, level, east_in[s][:, 0:1], south_in[s][0:1, :], depth, opened
            )
            st[0] = level
            st[1] = fluxes[0]
            st[2] = fluxes[1]

            wait_all(ret_in.at[s], ret_recv.at[s])
            ret_now[...] = ret_in[s]
            lane = iota((PH, width), 1)
            for band in range(K):
                first = band * FINE_ROWS + TOP
                merged = [st[f, first : first + PH, :] for f in range(3)]
                for j in range(RR - 1):
                    p = band * (RR - 1) + j
                    column = LEFT + j * PW
                    block = ret_now[slots[p]]
                    mask = (
                        (lane >= column)
                        & (lane < column + PW)
                        & (jnp.full((PH, width), covers[p], jnp.int32) > 0)
                    )
                    for f in range(3):
                        shifted = pltpu.roll(block, (column - f * PW) % width, 1)
                        merged[f] = jnp.where(mask, shifted, merged[f])
                for f in range(3):
                    st[f, first : first + PH, :] = merged[f]

        out_ref[0] = st[...]

        for s in range(STEPS):

            @pl.when(has_east)
            def _():
                halo(s, 0, east_out.at[s], west_in.at[s], east).wait_send()

            @pl.when(has_south)
            def _():
                halo(s, 1, south_out.at[s], north_in.at[s], south).wait_send()

            @pl.when(has_west)
            def _():
                halo(s, 2, level_out.at[s], east_in.at[s], west).wait_send()

            @pl.when(has_north)
            def _():
                halo(s, 3, level_out.at[s, pl.ds(0, 8)], south_in.at[s], north).wait_send()

        for s in range(STEPS + 1):
            wait_all(strips_in.at[s], strip_send.at[s])

    @pl.when(jnp.logical_not(is_outer))
    def _():
        st[...] = state_ref[0]
        spots, lives = [], []
        for k in range(K):
            spot, live = jnp.int32(0), jnp.int32(0)
            for n in range(nests):
                hit = host_ref[n] == tile * K + k
                spot = jnp.where(hit, place_ref[n], spot)
                live = jnp.where(hit, 1, live)
            spots.append(spot)
            lives.append(live)
        homes = [spot // NPOS for spot in spots]
        bands = [lax.rem(spot, NPOS) // (RR - 1) for spot in spots]
        columns = [lax.rem(spot, RR - 1) for spot in spots]
        for k in range(K):
            source = iota((width, width), 0)
            fine = iota((width, width), 1)
            wanted = LEFT + columns[k] * PW + fine // RR
            spread[k] = (source == wanted).astype(jnp.float32)
        grow = (iota((FINE_ROWS, PH), 0) // RR == iota((FINE_ROWS, PH), 1)).astype(jnp.float32)
        gather_from = iota((3 * width, width), 0)
        gather_to = iota((3 * width, width), 1)
        field, lane_in = gather_from // width, lax.rem(gather_from, width)
        weight = jnp.where(
            field == 1, jnp.where(lax.rem(lane_in, RR) == RR - 1, 1.0, 0.0), 1.0 / RR
        )
        gather = jnp.where(gather_to == field * PW + lane_in // RR, weight, 0.0)
        shrink_row = iota((2 * PH, FINE_ROWS), 0)
        shrink_from = iota((2 * PH, FINE_ROWS), 1)
        shrink = jnp.where(
            shrink_row < PH,
            jnp.where(shrink_from // RR == shrink_row, 1.0 / RR, 0.0),
            jnp.where(shrink_from == (shrink_row - PH) * RR + RR - 1, 1.0, 0.0),
        )

        def side_ghosts(block, k):
            lane, sub = iota((PH, width), 1), iota((PH, width), 0)
            tall_lane = iota((FINE_ROWS, width), 1)
            tall = dot(grow, block)
            wide = dot(block, spread[k])
            west_lane = bands[k] * (2 * (RR - 1)) + columns[k]
            west = jnp.sum(jnp.where(tall_lane == west_lane, tall, 0.0), axis=1, keepdims=True)
            east = jnp.sum(
                jnp.where(tall_lane == west_lane + (RR - 1), tall, 0.0), axis=1, keepdims=True
            )
            north = jnp.sum(jnp.where(sub == 2 * bands[k], wide, 0.0), axis=0, keepdims=True)
            south = jnp.sum(jnp.where(sub == 2 * bands[k] + 1, wide, 0.0), axis=0, keepdims=True)
            return west, north, east, south

        def keep(k, sides):
            west, north, east, south = sides
            lane = iota((FINE_ROWS, width), 1)
            ghosts[k, 0:FINE_ROWS] = jnp.where(lane == 0, west, east)
            ghosts[k, FINE_ROWS : FINE_ROWS + 8] = jnp.where(
                iota((8, width), 0) == 0, north, south
            )

        def kept(k):
            return (
                ghosts[k, 0:FINE_ROWS][:, 0:1],
                ghosts[k, FINE_ROWS : FINE_ROWS + 1],
                ghosts[k, 0:FINE_ROWS][:, 1:2],
                ghosts[k, FINE_ROWS + 1 : FINE_ROWS + 2],
            )

        pl.semaphore_wait(barrier, tiles)
        wait_all(strips_in.at[0], strip_recv.at[0])
        strips_now[...] = strips_in[0]
        for k in range(K):
            keep(k, side_ghosts(strips_now[homes[k]], k))

        @pl.loop(0, STEPS)
        def _(s):
            wait_all(strips_in.at[s + 1], strip_recv.at[s + 1])
            strips_now[...] = strips_in[s + 1]
            for k in range(K):
                slot = pl.ds(k * FINE_ROWS, FINE_ROWS)
                old = kept(k)
                new = side_ghosts(strips_now[homes[k]], k)
                surface, eastward, southward = st[0, slot], st[1, slot], st[2, slot]
                depth = [depth_ref[0, i, slot] for i in range(2)]
                opened = [open_ref[0, i, slot].astype(jnp.float32) for i in range(2)]
                for m in range(1, RR + 1):
                    west_g, north_g, east_g, south_g = [
                        a + (m / RR) * (b - a) for a, b in zip(old, new)
                    ]
                    surface = new_level(surface, eastward, southward, west_g, north_g)
                    eastward, southward = new_fluxes(
                        eastward, southward, surface, east_g, south_g, depth, opened
                    )
                st[0, slot] = surface
                st[1, slot] = eastward
                st[2, slot] = southward
                packed = dot(jnp.concatenate([surface, eastward, southward], axis=1), gather)
                both = dot(shrink, packed)
                ret_out[s, k] = jnp.where(
                    iota((PH, width), 1) < 2 * PW, both[0:PH], both[PH : 2 * PH]
                )
                keep(k, new)
            send_all(ret_out.at[s], ret_in.at[s, pl.ds(tile * K, K)], ret_send.at[s], ret_recv.at[s])

        for k in range(K):
            slot = pl.ds(k * FINE_ROWS, FINE_ROWS)
            live = jnp.full((FINE_ROWS, width), lives[k], jnp.int32) > 0
            for f in range(3):
                out_ref[0, f, slot] = jnp.where(live, st[f, slot], state_ref[0, f, slot])

        for s in range(STEPS):
            wait_all(ret_in.at[s], ret_send.at[s])


def on_device(n_row, n_nest, ocean_state, face_depth, face_open, nest_place, nest_host):
    tiles = n_row * n_nest
    height, width = ocean_state.shape[2:]
    f32 = jnp.float32
    vmem = pl.BlockSpec(memory_space=pltpu.VMEM)
    smem = pl.BlockSpec(memory_space=pltpu.SMEM)
    dma = pltpu.SemaphoreType.DMA
    return pl.pallas_call(
        functools.partial(kernel, n_row, n_nest),
        out_shape=jax.ShapeDtypeStruct(ocean_state.shape, f32),
        in_specs=[smem, smem, vmem, vmem, vmem],
        out_specs=vmem,
        scratch_shapes=[
            pltpu.VMEM((3, height, width), f32),
            pltpu.VMEM((3, height, width), f32),
            pltpu.VMEM((STEPS + 1, PH, width), f32),
            pltpu.VMEM((STEPS + 1, tiles, PH, width), f32),
            pltpu.VMEM((STEPS, K, PH, width), f32),
            pltpu.VMEM((STEPS, tiles * K, PH, width), f32),
            pltpu.VMEM((STEPS, height, width), f32),
            pltpu.VMEM((STEPS, 8, width), f32),
            pltpu.VMEM((STEPS, height, width), f32),
            pltpu.VMEM((STEPS, height, width), f32),
            pltpu.VMEM((STEPS, 8, width), f32),
            pltpu.VMEM((STEPS, height, width), f32),
            pltpu.VMEM((STEPS, 8, width), f32),
            pltpu.VMEM((K, width, width), f32),
            pltpu.VMEM((K, FINE_ROWS + 8, width), f32),
            pltpu.VMEM((tiles, PH, width), f32),
            pltpu.VMEM((tiles * K, PH, width), f32),
            dma((STEPS + 1,)),
            dma((STEPS + 1,)),
            dma((STEPS,)),
            dma((STEPS,)),
            dma((STEPS, 4)),
            dma((STEPS, 4)),
        ],
        compiler_params=pltpu.CompilerParams(collective_id=0, has_side_effects=True),
    )(nest_place, nest_host, ocean_state, face_depth, face_open)


def solution(mesh):
    field = P("sec", None, "row", "nest")
    return jax.shard_map(
        functools.partial(on_device, mesh.shape["row"], mesh.shape["nest"]),
        mesh=mesh,
        in_specs=(field, field, field, P(), P()),
        out_specs=field,
        check_vma=False,
    )
```

time: 230 us -> 55.8 us (0.24)
  waiting for transfers between devices: 70.2 us -> 0 us
  starting transfers between devices: 64.2 us -> 0 us
  blocking collectives: 55.3 us -> 0 us
  Pallas kernels: 0 us -> 54.1 us
  local copies, waits for them, and re-layouts: 24.8 us -> 1.54 us
  other arithmetic: 10.4 us -> 0 us
  matrix products: 2.83 us -> 0 us
    all_to_all x3 -> x0, blocking collectives: 55.3 us -> none  [route_returns(): lax.all_to_all(outgoing, ('sec', 'row', 'nest'), split_axis=0, concat_axi...]
    pallas_call x0 -> x1, Pallas kernels: none -> 54.1 us  [on_device(): pl.pallas_call(functools.partial(kernel, n_row, n_nest), out_shape=jax.Sh...]
    all_to_all x6 -> x0, waiting for transfers between devices: 36.5 us -> none  [the longest x5 27.1 us: route_strips(): lax.all_to_all(widened, ('sec', 'row', 'nest'), split_axis=0, concat_axis...]
    ppermute x16 -> x0, starting transfers between devices: 34.2 us -> none  [the longest x8 23.9 us: padded_2(): before = lax.ppermute(last, axis, up)]
    ppermute x16 -> x0, waiting for transfers between devices: 33.7 us -> none  [the longest x8 29.6 us: padded_2(): after = lax.ppermute(leading, axis, down)]
    all_to_all x6 -> x0, starting transfers between devices: 30 us -> none  [the longest x5 20.7 us: route_strips(): lax.all_to_all(widened, ('sec', 'row', 'nest'), split_axis=0, concat_axis...]
    scatter x4 -> x0, local copies, waits for them, and re-layouts: 8.47 us -> none  [apply_feedback(): banded.at[:, :, top_rows:top_rows + PH, left_cols:left_cols + span_cols]]
    unnamed x29 -> x1, local copies, waits for them, and re-layouts: 9.51 us -> 1.54 us
  transfers between devices with their start and end apart: 22 -> 0, of which waited for: 16 -> 0; matrix products, arithmetic and copies ran while one was open for 3% -> 0% of each run, Pallas kernels for 0% -> 0%
where the time goes in v1:
time: 55.8 us; the launch traced here: 55.6 us
  Pallas kernels  54.1 us (97%)
  local copies, waits for them, and re-layouts  1.54 us (3%)
    pallas_call x1, Pallas kernels, on_device(): pl.pallas_call(functools.partial(kernel, n_row, n_nest), out_shape=jax.Sh...  54.1 us
    unnamed x1, local copies, waits for them, and re-layouts  1.54 us

profile of v1, /device:TPU:0, one launch (start us, length us, event | category | flops | bytes accessed | tf_op | source)
XLA Modules:
  0.0 55.6 jit_solution(7566824593978956037)
XLA Ops:
  0.0 54.1 %shard_map.55 = f32[1,3,64,128]{3,2,1,0:T(8,128)} custom-call(s32[16]{0:T(128)} %place_ref.1, s32[16]{0:T(128)} %host_ref.1, f32[1,3,64,128]{3,2,1,0:T(8,128)} %state_ref.1, f32[1,2,64,128]{3,2,1,0:T(8,128)} %depth_ref.1, s32[1,2,64,128]{3,2,1,0:T(8,128)} %open_ref.1), custom_call_target="tpu_custom_call" | custom-call | tf_op jit(solution)/shard_map/pallas_call | solution.py:433
  54.1 1.5 %copy.7 = f32[1,3,64,128]{3,2,1,0:T(8,128)} copy(f32[1,3,64,128]{3,2,1,0:T(8,128)} %shard_map.55) | data formatting | bytes 196608

commit v2 on v1

--- a/solution.py
+++ b/solution.py
@@ -19,6 +19,7 @@
 FINE_ROWS = RR * PH
 TOP = (RR - 1) * PH // 2
 LEFT = PW // 2
+EDGES = ((0, PW - 1), (1, PW - 1), (1, PW - 2), (2, PW - 1), (0, 0), (1, 0), (2, 0))
 
 
 def iota(shape, dim):
@@ -75,6 +76,30 @@
     return block
 
 
+def pack_ring(sides, lines):
+    ref, width = sides[0][0], sides[0][0].shape[-1]
+    lane, sub = iota((PH, width), 1), iota((PH, width), 0)
+    span = (RR - 1) * PW
+    block = jnp.zeros((PH, width), jnp.float32)
+    inner = (lane >= LEFT) & (lane < LEFT + span)
+    for band in range(K):
+        first = band * FINE_ROWS + TOP
+        base = band * (LEFT + span)
+        for i, (ref, index, shift) in enumerate(sides):
+            values = ref[index + (slice(first, first + PH), slice(None))].astype(jnp.float32)
+            for j in range(RR - 1):
+                target = base + 3 * j + i
+                source = LEFT + j * PW + shift
+                block = jnp.where(
+                    lane == target, pltpu.roll(values, (target - source) % width, 1), block
+                )
+        for i, (ref, index, shift) in enumerate(lines):
+            at = first + shift
+            line = ref[index + (slice(at, at + 1), slice(None))].astype(jnp.float32)
+            block = jnp.where(inner & (sub == 3 * band + i), line, block)
+    return block
+
+
 def kernel(
     n_row,
     n_nest,
@@ -86,8 +111,14 @@
     out_ref,
     st,
     tmp,
-    strips_out,
-    strips_in,
+    first_out,
+    first_in,
+    fixed_out,
+    fixed_in,
+    ring_out,
+    ring_in,
+    edge_out,
+    edge_in,
     ret_out,
     ret_in,
     east_out,
@@ -99,10 +130,16 @@
     south_in,
     spread,
     ghosts,
-    strips_now,
+    ring_now,
+    edge_now,
     ret_now,
-    strip_send,
-    strip_recv,
+    fixed_terms,
+    first_sems,
+    fixed_sems,
+    ring_send,
+    ring_recv,
+    edge_send,
+    edge_recv,
     ret_send,
     ret_recv,
     halo_send,
@@ -129,18 +166,21 @@
             barrier, inc=1, device_id=(1 - sec, t // n_nest, lax.rem(t, n_nest)), device_id_type=MESH
         )
 
-    def send_all(src, dst_of, send_sem, recv_sem):
-        @pl.loop(0, tiles)
+    def send_to(section, count, src, dst, send_sem, recv_sem):
+        @pl.loop(0, count)
         def _(i):
             t = lax.rem(tile + i + 1, tiles)
             pltpu.make_async_remote_copy(
                 src_ref=src,
-                dst_ref=dst_of,
+                dst_ref=dst,
                 send_sem=send_sem,
                 recv_sem=recv_sem,
-                device_id=(1 - sec, t // n_nest, lax.rem(t, n_nest)),
+                device_id=(section, t // n_nest, lax.rem(t, n_nest)),
                 device_id_type=MESH,
             ).start()
+
+    def send_all(src, dst, send_sem, recv_sem):
+        send_to(1 - sec, tiles, src, dst, send_sem, recv_sem)
 
     def wait_all(whole, sem):
         pltpu.make_async_copy(whole, whole, sem).wait()
@@ -183,9 +223,6 @@
             peers = peers + jnp.where(present, 1, 0)
         pl.semaphore_wait(barrier, peers)
 
-        strips_out[0] = pack_strips(st)
-        send_all(strips_out.at[0], strips_in.at[0, tile], strip_send.at[0], strip_recv.at[0])
-
         def halo(s, kind, src, dst, device):
             return pltpu.make_async_remote_copy(
                 src_ref=src,
@@ -204,13 +241,35 @@
             tmp[0] = level
             tmp[1] = fluxes[0]
             tmp[2] = fluxes[1]
-            strips_out[s + 1] = pack_strips(tmp)
-            send_all(
-                strips_out.at[s + 1],
-                strips_in.at[s + 1, tile],
-                strip_send.at[s + 1],
-                strip_recv.at[s + 1],
-            )
+
+            @pl.when(s == 0)
+            def _():
+                first_out[0] = pack_strips(st)
+                first_out[1] = pack_strips(tmp)
+                send_all(first_out, first_in.at[tile], first_sems.at[0], first_sems.at[1])
+
+            @pl.when(s < STEPS - 1)
+            def _():
+                cols = iota((height, width), 1)
+                rows = iota((height, width), 0)
+                east_gap = fluxes[0] - jnp.where(cols == 0, 0.0, pltpu.roll(fluxes[0], 1, 1))
+                south_gap = fluxes[1] - jnp.where(rows == 0, 0.0, pltpu.roll(fluxes[1], 1, 0))
+                tmp[3] = level - COURANT * (east_gap + south_gap)
+                tmp[4] = level - COURANT * (fluxes[0] + south_gap)
+                tmp[5] = level - COURANT * (east_gap + fluxes[1])
+                ring_out[s] = pack_ring(
+                    [(tmp, (3,), -1), (tmp, (1,), -1), (tmp, (4,), PW)],
+                    [(tmp, (3,), -1), (tmp, (2,), -1), (tmp, (5,), PH)],
+                )
+                send_all(ring_out.at[s], ring_in.at[s, tile], ring_send.at[s], ring_recv.at[s])
+
+            @pl.when(s == 0)
+            def _():
+                fixed_out[...] = pack_ring(
+                    [(depth_ref, (0, 0), -1), (open_ref, (0, 0), -1)],
+                    [(depth_ref, (0, 1), -1), (open_ref, (0, 1), -1)],
+                )
+                send_all(fixed_out, fixed_in.at[tile], fixed_sems.at[0], fixed_sems.at[1])
 
             east_out[s] = eastward
             south_out[s] = southward[height - 8 :]
@@ -308,11 +367,20 @@
             def _():
                 halo(s, 3, level_out.at[s, pl.ds(0, 8)], south_in.at[s], north).wait_send()
 
-        for s in range(STEPS + 1):
-            wait_all(strips_in.at[s], strip_send.at[s])
+        wait_all(first_in, first_sems.at[0])
+        wait_all(fixed_in, fixed_sems.at[0])
+        for s in range(STEPS - 1):
+            wait_all(ring_in.at[s], ring_send.at[s])
 
     @pl.when(jnp.logical_not(is_outer))
     def _():
+        @pl.loop(0, tiles - 1)
+        def _(i):
+            t = lax.rem(tile + i + 1, tiles)
+            pl.semaphore_signal(
+                barrier, inc=1, device_id=(sec, t // n_nest, lax.rem(t, n_nest)), device_id_type=MESH
+            )
+
         st[...] = state_ref[0]
         spots, lives = [], []
         for k in range(K):
@@ -326,6 +394,18 @@
         homes = [spot // NPOS for spot in spots]
         bands = [lax.rem(spot, NPOS) // (RR - 1) for spot in spots]
         columns = [lax.rem(spot, RR - 1) for spot in spots]
+        near = []
+        for k in range(K):
+            pair = []
+            for side in (-1, 1):
+                inside = (columns[k] + side >= 0) & (columns[k] + side < RR - 1)
+                slot, cover = jnp.int32(0), jnp.int32(0)
+                for n in range(nests):
+                    hit = inside & (place_ref[n] == spots[k] + side)
+                    slot = jnp.where(hit, host_ref[n], slot)
+                    cover = jnp.where(hit, 1, cover)
+                pair.append((slot // K, lax.rem(slot, K), cover))
+            near.append(pair)
         for k in range(K):
             source = iota((width, width), 0)
             fine = iota((width, width), 1)
@@ -339,6 +419,15 @@
             field == 1, jnp.where(lax.rem(lane_in, RR) == RR - 1, 1.0, 0.0), 1.0 / RR
         )
         gather = jnp.where(gather_to == field * PW + lane_in // RR, weight, 0.0)
+        for i, (f, c) in enumerate(EDGES):
+            gather = gather + jnp.where(
+                (gather_to == 3 * PW + i) & (field == f) & (lane_in // RR == c), weight, 0.0
+            )
+        widen_to = iota((width, 3 * width), 1)
+        widen = (
+            iota((width, 3 * width), 0)
+            == (widen_to // width) * PW + lax.rem(widen_to, width) // RR
+        ).astype(jnp.float32)
         shrink_row = iota((2 * PH, FINE_ROWS), 0)
         shrink_from = iota((2 * PH, FINE_ROWS), 1)
         shrink = jnp.where(
@@ -361,36 +450,96 @@
             south = jnp.sum(jnp.where(sub == 2 * bands[k] + 1, wide, 0.0), axis=0, keepdims=True)
             return west, north, east, south
 
-        def keep(k, sides):
+        def keep(buffer, k, sides):
             west, north, east, south = sides
             lane = iota((FINE_ROWS, width), 1)
-            ghosts[k, 0:FINE_ROWS] = jnp.where(lane == 0, west, east)
-            ghosts[k, FINE_ROWS : FINE_ROWS + 8] = jnp.where(
+            buffer[k, 0:FINE_ROWS] = jnp.where(lane == 0, west, east)
+            buffer[k, FINE_ROWS : FINE_ROWS + 8] = jnp.where(
                 iota((8, width), 0) == 0, north, south
             )
 
-        def kept(k):
+        def kept(buffer, k):
             return (
-                ghosts[k, 0:FINE_ROWS][:, 0:1],
-                ghosts[k, FINE_ROWS : FINE_ROWS + 1],
-                ghosts[k, 0:FINE_ROWS][:, 1:2],
-                ghosts[k, FINE_ROWS + 1 : FINE_ROWS + 2],
-            )
-
-        pl.semaphore_wait(barrier, tiles)
-        wait_all(strips_in.at[0], strip_recv.at[0])
-        strips_now[...] = strips_in[0]
+                buffer[k, 0:FINE_ROWS][:, 0:1],
+                buffer[k, FINE_ROWS : FINE_ROWS + 1],
+                buffer[k, 0:FINE_ROWS][:, 1:2],
+                buffer[k, FINE_ROWS + 1 : FINE_ROWS + 2],
+            )
+
+        def pick_lane(tall, index):
+            lane = iota(tall.shape, 1)
+            return jnp.sum(jnp.where(lane == index, tall, 0.0), axis=1, keepdims=True)
+
+        def pick_row(wide, index):
+            sub = iota(wide.shape, 0)
+            return jnp.sum(jnp.where(sub == index, wide, 0.0), axis=0, keepdims=True)
+
+        def next_sides(k):
+            ring = ring_now[homes[k]]
+            tall, wide = dot(grow, ring), dot(ring, spread[k])
+            base = bands[k] * (LEFT + (RR - 1) * PW) + 3 * columns[k]
+            level_w, flux_w, level_e = [pick_lane(tall, base + i) for i in range(3)]
+            level_n, flux_n, level_s = [pick_row(wide, 3 * bands[k] + i) for i in range(3)]
+            flux_line = pick_row(ring, 3 * bands[k] + 1)
+            first = LEFT + columns[k] * PW
+            own = dot(dot(grow, ret_now[k]), widen)
+            surface, eastward, southward = [own[:, f * width : (f + 1) * width] for f in range(3)]
+            depth_w, depth_n, open_w, open_n = kept(fixed_terms, k)
+
+            taken = []
+            for device, slot, cover in near[k]:
+                edges = edge_now[device]
+                chosen = edges
+                for other in range(1, K):
+                    chosen = jnp.where(
+                        jnp.full(edges.shape, slot, jnp.int32) == other,
+                        pltpu.roll(edges, width - 8 * other, 1),
+                        chosen,
+                    )
+                taken.append((dot(grow, chosen), jnp.full((FINE_ROWS, 1), cover, jnp.int32) > 0))
+            (left, has_left), (right, has_right) = taken
+            s_l, e_l, e_p, q_l = [left[:, i : i + 1] for i in range(4)]
+            s_f, e_f, q_f = [right[:, i : i + 1] for i in range(4, 7)]
+            left_level = s_l - COURANT * ((e_l - e_p) + (q_l - below(q_l, pick_lane(flux_line, first - 1))))
+            right_level = s_f - COURANT * (e_f + (q_f - below(q_f, pick_lane(flux_line, first + PW))))
+            level_w = jnp.where(has_left, left_level, level_w)
+            flux_w = jnp.where(has_left, e_l, flux_w)
+            level_e = jnp.where(has_right, right_level, level_e)
+
+            cols, rows = iota((FINE_ROWS, width), 1), iota((FINE_ROWS, width), 0)
+            behind = jnp.where(cols < RR, flux_w, pltpu.roll(eastward, RR, 1))
+            above = jnp.where(rows < RR, flux_n, pltpu.roll(southward, RR, 0))
+            level = surface - COURANT * ((eastward - behind) + (southward - above))
+            west_cell = level[:, 0:1]
+            north_cell = level[0:1, :]
+            west = open_w * (
+                flux_w - COURANT * (depth_w + 0.5 * (level_w + west_cell)) * (west_cell - level_w)
+            )
+            north = open_n * (
+                flux_n - COURANT * (depth_n + 0.5 * (level_n + north_cell)) * (north_cell - level_n)
+            )
+            east = level_e + COURANT * eastward[:, width - 1 : width]
+            south = level_s + COURANT * southward[FINE_ROWS - 1 : FINE_ROWS, :]
+            return west, north, east, south
+
+        def below(column, top):
+            wide = jnp.broadcast_to(column, (FINE_ROWS, width))
+            rows = iota((FINE_ROWS, width), 0)
+            return jnp.where(rows < RR, top, pltpu.roll(wide, RR, 0))[:, 0:1]
+
+        pl.semaphore_wait(barrier, 2 * tiles - 1)
+        wait_all(first_in, first_sems.at[1])
         for k in range(K):
-            keep(k, side_ghosts(strips_now[homes[k]], k))
+            keep(ghosts.at[0], k, side_ghosts(first_in[homes[k], 0], k))
+            keep(ghosts.at[1], k, side_ghosts(first_in[homes[k], 1], k))
 
         @pl.loop(0, STEPS)
         def _(s):
-            wait_all(strips_in.at[s + 1], strip_recv.at[s + 1])
-            strips_now[...] = strips_in[s + 1]
+            edge = jnp.zeros((PH, width), jnp.float32)
+            lane = iota((PH, width), 1)
             for k in range(K):
                 slot = pl.ds(k * FINE_ROWS, FINE_ROWS)
-                old = kept(k)
-                new = side_ghosts(strips_now[homes[k]], k)
+                old, new = kept(ghosts.at[0], k), kept(ghosts.at[1], k)
                 surface, eastward, southward = st[0, slot], st[1, slot], st[2, slot]
                 depth = [depth_ref[0, i, slot] for i in range(2)]
                 opened = [open_ref[0, i, slot].astype(jnp.float32) for i in range(2)]
@@ -407,11 +556,51 @@
                 st[2, slot] = southward
                 packed = dot(jnp.concatenate([surface, eastward, southward], axis=1), gather)
                 both = dot(shrink, packed)
-                ret_out[s, k] = jnp.where(
-                    iota((PH, width), 1) < 2 * PW, both[0:PH], both[PH : 2 * PH]
-                )
-                keep(k, new)
+                mean = lane < 2 * PW
+                for i, (f, c) in enumerate(EDGES):
+                    if f < 2:
+                        mean = mean | (lane == 3 * PW + i)
+                both = jnp.where(mean, both[0:PH], both[PH : 2 * PH])
+                ret_out[s, k] = both
+                ret_now[k] = both
+                shifted = pltpu.roll(both, (8 * k - 3 * PW) % width, 1)
+                edge = jnp.where((lane >= 8 * k) & (lane < 8 * k + 8), shifted, edge)
+
+            @pl.when(s < STEPS - 1)
+            def _():
+                edge_out[s] = edge
+                send_to(1, tiles - 1, edge_out.at[s], edge_in.at[s, tile], edge_send.at[s], edge_recv.at[s])
+
             send_all(ret_out.at[s], ret_in.at[s, pl.ds(tile * K, K)], ret_send.at[s], ret_recv.at[s])
+
+            @pl.when(s == 0)
+            def _():
+                wait_all(fixed_in, fixed_sems.at[1])
+                for k in range(K):
+                    fixed = fixed_in[homes[k]]
+                    tall, wide = dot(grow, fixed), dot(fixed, spread[k])
+                    base = bands[k] * (LEFT + (RR - 1) * PW) + 3 * columns[k]
+                    keep(
+                        fixed_terms,
+                        k,
+                        (
+                            pick_lane(tall, base),
+                            pick_row(wide, 3 * bands[k]),
+                            pick_lane(tall, base + 1),
+                            pick_row(wide, 3 * bands[k] + 1),
+                        ),
+                    )
+
+            @pl.when(s < STEPS - 1)
+            def _():
+                wait_all(ring_in.at[s], ring_recv.at[s])
+                ring_now[...] = ring_in[s]
+                wait_all(edge_in.at[s, pl.ds(0, tiles - 1)], edge_recv.at[s])
+                edge_now[...] = edge_in[s]
+                edge_now[tile] = edge
+                for k in range(K):
+                    ghosts[0, k] = ghosts[1, k]
+                    keep(ghosts.at[1], k, next_sides(k))
 
         for k in range(K):
             slot = pl.ds(k * FINE_ROWS, FINE_ROWS)
@@ -421,6 +610,8 @@
 
         for s in range(STEPS):
             wait_all(ret_in.at[s], ret_send.at[s])
+        for s in range(STEPS - 1):
+            wait_all(edge_in.at[s, pl.ds(0, tiles - 1)], edge_send.at[s])
 
 
 def on_device(n_row, n_nest, ocean_state, face_depth, face_open, nest_place, nest_host):
@@ -437,9 +628,15 @@
         out_specs=vmem,
         scratch_shapes=[
             pltpu.VMEM((3, height, width), f32),
-            pltpu.VMEM((3, height, width), f32),
-            pltpu.VMEM((STEPS + 1, PH, width), f32),
-            pltpu.VMEM((STEPS + 1, tiles, PH, width), f32),
+            pltpu.VMEM((6, height, width), f32),
+            pltpu.VMEM((2, PH, width), f32),
+            pltpu.VMEM((tiles, 2, PH, width), f32),
+            pltpu.VMEM((PH, width), f32),
+            pltpu.VMEM((tiles, PH, width), f32),
+            pltpu.VMEM((STEPS - 1, PH, width), f32),
+            pltpu.VMEM((STEPS - 1, tiles, PH, width), f32),
+            pltpu.VMEM((STEPS - 1, PH, width), f32),
+            pltpu.VMEM((STEPS - 1, tiles, PH, width), f32),
             pltpu.VMEM((STEPS, K, PH, width), f32),
             pltpu.VMEM((STEPS, tiles * K, PH, width), f32),
             pltpu.VMEM((STEPS, height, width), f32),
@@ -450,11 +647,17 @@
             pltpu.VMEM((STEPS, height, width), f32),
             pltpu.VMEM((STEPS, 8, width), f32),
             pltpu.VMEM((K, width, width), f32),
-            pltpu.VMEM((K, FINE_ROWS + 8, width), f32),
+            pltpu.VMEM((2, K, FINE_ROWS + 8, width), f32),
+            pltpu.VMEM((tiles, PH, width), f32),
             pltpu.VMEM((tiles, PH, width), f32),
             pltpu.VMEM((tiles * K, PH, width), f32),
-            dma((STEPS + 1,)),
-            dma((STEPS + 1,)),
+            pltpu.VMEM((K, FINE_ROWS + 8, width), f32),
+            dma((2,)),
+            dma((2,)),
+            dma((STEPS - 1,)),
+            dma((STEPS - 1,)),
+            dma((STEPS - 1,)),
+            dma((STEPS - 1,)),
             dma((STEPS,)),
             dma((STEPS,)),
             dma((STEPS, 4)),

time: 55.8 us -> 43.4 us (0.78)
  Pallas kernels: 54.1 us -> 41.6 us
    pallas_call x1, Pallas kernels: 54.1 us -> 41.6 us  [on_device(): pl.pallas_call(functools.partial(kernel, n_row, n_nest), out_shape=jax.Sh...]
where the time goes in v2:
time: 43.4 us; the launch traced here: 43.2 us
  Pallas kernels  41.6 us (96%)
  local copies, waits for them, and re-layouts  1.54 us (4%)
    pallas_call x1, Pallas kernels, on_device(): pl.pallas_call(functools.partial(kernel, n_row, n_nest), out_shape=jax.Sh...  41.6 us
    unnamed x1, local copies, waits for them, and re-layouts  1.54 us

profile of v2, /device:TPU:0, one launch (start us, length us, event | category | flops | bytes accessed | tf_op | source)
XLA Modules:
  0.0 43.2 jit_solution(8475528231070405572)
XLA Ops:
  0.0 41.6 %shard_map.55 = f32[1,3,64,128]{3,2,1,0:T(8,128)} custom-call(s32[16]{0:T(128)} %place_ref.1, s32[16]{0:T(128)} %host_ref.1, f32[1,3,64,128]{3,2,1,0:T(8,128)} %state_ref.1, f32[1,2,64,128]{3,2,1,0:T(8,128)} %depth_ref.1, s32[1,2,64,128]{3,2,1,0:T(8,128)} %open_ref.1), custom_call_target="tpu_custom_call" | custom-call | tf_op jit(solution)/shard_map/pallas_call | solution.py:624
  41.6 1.5 %copy.7 = f32[1,3,64,128]{3,2,1,0:T(8,128)} copy(f32[1,3,64,128]{3,2,1,0:T(8,128)} %shard_map.55) | data formatting | bytes 196608

commit v3 on v2

--- a/solution.py
+++ b/solution.py
@@ -167,17 +167,24 @@
         )
 
     def send_to(section, count, src, dst, send_sem, recv_sem):
-        @pl.loop(0, count)
+        @pl.loop(0, tiles)
         def _(i):
-            t = lax.rem(tile + i + 1, tiles)
-            pltpu.make_async_remote_copy(
-                src_ref=src,
-                dst_ref=dst,
-                send_sem=send_sem,
-                recv_sem=recv_sem,
-                device_id=(section, t // n_nest, lax.rem(t, n_nest)),
-                device_id_type=MESH,
-            ).start()
+            t = lax.rem(2 * tiles - 1 - tile - i, tiles)
+
+            def go():
+                pltpu.make_async_remote_copy(
+                    src_ref=src,
+                    dst_ref=dst,
+                    send_sem=send_sem,
+                    recv_sem=recv_sem,
+                    device_id=(section, t // n_nest, lax.rem(t, n_nest)),
+                    device_id_type=MESH,
+                ).start()
+
+            if count == tiles:
+                go()
+            else:
+                pl.when(t != tile)(go)
 
     def send_all(src, dst, send_sem, recv_sem):
         send_to(1 - sec, tiles, src, dst, send_sem, recv_sem)
@@ -218,11 +225,6 @@
                 for s in range(STEPS):
                     buffer[s] = jnp.zeros(buffer.shape[1:], jnp.float32)
 
-        peers = jnp.int32(tiles)
-        for present, _device in links:
-            peers = peers + jnp.where(present, 1, 0)
-        pl.semaphore_wait(barrier, peers)
-
         def halo(s, kind, src, dst, device):
             return pltpu.make_async_remote_copy(
                 src_ref=src,
@@ -246,6 +248,10 @@
             def _():
                 first_out[0] = pack_strips(st)
                 first_out[1] = pack_strips(tmp)
+                peers = jnp.int32(tiles)
+                for present, _device in links:
+                    peers = peers + jnp.where(present, 1, 0)
+                pl.semaphore_wait(barrier, peers)
                 send_all(first_out, first_in.at[tile], first_sems.at[0], first_sems.at[1])
 
             @pl.when(s < STEPS - 1)
@@ -412,8 +418,8 @@
             wanted = LEFT + columns[k] * PW + fine // RR
             spread[k] = (source == wanted).astype(jnp.float32)
         grow = (iota((FINE_ROWS, PH), 0) // RR == iota((FINE_ROWS, PH), 1)).astype(jnp.float32)
-        gather_from = iota((3 * width, width), 0)
-        gather_to = iota((3 * width, width), 1)
+        gather_from = iota((3 * width, 2 * width), 0)
+        gather_to = iota((3 * width, 2 * width), 1)
         field, lane_in = gather_from // width, lax.rem(gather_from, width)
         weight = jnp.where(
             field == 1, jnp.where(lax.rem(lane_in, RR) == RR - 1, 1.0, 0.0), 1.0 / RR
@@ -421,8 +427,17 @@
         gather = jnp.where(gather_to == field * PW + lane_in // RR, weight, 0.0)
         for i, (f, c) in enumerate(EDGES):
             gather = gather + jnp.where(
-                (gather_to == 3 * PW + i) & (field == f) & (lane_in // RR == c), weight, 0.0
-            )
+                (gather_to >= width)
+                & (lax.rem(gather_to, 8 * K) == i)
+                & (field == f)
+                & (lane_in // RR == c),
+                weight,
+                0.0,
+            )
+        fold_to = iota((width, width), 1)
+        fold = (
+            (lax.rem(iota((width, width), 0), 8 * K) == fold_to) & (fold_to < 8 * K)
+        ).astype(jnp.float32)
         widen_to = iota((width, 3 * width), 1)
         widen = (
             iota((width, 3 * width), 0)
@@ -474,21 +489,27 @@
             sub = iota(wide.shape, 0)
             return jnp.sum(jnp.where(sub == index, wide, 0.0), axis=0, keepdims=True)
 
-        def next_sides(k):
+        def ring_terms(k):
             ring = ring_now[homes[k]]
             tall, wide = dot(grow, ring), dot(ring, spread[k])
             base = bands[k] * (LEFT + (RR - 1) * PW) + 3 * columns[k]
-            level_w, flux_w, level_e = [pick_lane(tall, base + i) for i in range(3)]
-            level_n, flux_n, level_s = [pick_row(wide, 3 * bands[k] + i) for i in range(3)]
+            sides = [pick_lane(tall, base + i) for i in range(3)]
+            lines = [pick_row(wide, 3 * bands[k] + i) for i in range(3)]
             flux_line = pick_row(ring, 3 * bands[k] + 1)
             first = LEFT + columns[k] * PW
-            own = dot(dot(grow, ret_now[k]), widen)
+            corners = [pick_lane(flux_line, first - 1), pick_lane(flux_line, first + PW)]
+            return sides, lines, corners
+
+        def next_sides(k, own, ring):
+            (level_w, flux_w, level_e), (level_n, flux_n, level_s), (corner_w, corner_e) = ring
             surface, eastward, southward = [own[:, f * width : (f + 1) * width] for f in range(3)]
             depth_w, depth_n, open_w, open_n = kept(fixed_terms, k)
 
             taken = []
             for device, slot, cover in near[k]:
-                edges = edge_now[device]
+                line = jnp.broadcast_to(edge_now[device, 0:1], (FINE_ROWS, width))
+                own_row = iota((FINE_ROWS, width), 1) // (8 * K) == iota((FINE_ROWS, width), 0) // RR
+                edges = dot(jnp.where(own_row, line, 0.0), fold)
                 chosen = edges
                 for other in range(1, K):
                     chosen = jnp.where(
@@ -496,12 +517,12 @@
                         pltpu.roll(edges, width - 8 * other, 1),
                         chosen,
                     )
-                taken.append((dot(grow, chosen), jnp.full((FINE_ROWS, 1), cover, jnp.int32) > 0))
+                taken.append((chosen, jnp.full((FINE_ROWS, 1), cover, jnp.int32) > 0))
             (left, has_left), (right, has_right) = taken
             s_l, e_l, e_p, q_l = [left[:, i : i + 1] for i in range(4)]
             s_f, e_f, q_f = [right[:, i : i + 1] for i in range(4, 7)]
-            left_level = s_l - COURANT * ((e_l - e_p) + (q_l - below(q_l, pick_lane(flux_line, first - 1))))
-            right_level = s_f - COURANT * (e_f + (q_f - below(q_f, pick_lane(flux_line, first + PW))))
+            left_level = s_l - COURANT * ((e_l - e_p) + (q_l - below(q_l, corner_w)))
+            right_level = s_f - COURANT * (e_f + (q_f - below(q_f, corner_e)))
             level_w = jnp.where(has_left, left_level, level_w)
             flux_w = jnp.where(has_left, e_l, flux_w)
             level_e = jnp.where(has_right, right_level, level_e)
@@ -556,20 +577,31 @@
                 st[2, slot] = southward
                 packed = dot(jnp.concatenate([surface, eastward, southward], axis=1), gather)
                 both = dot(shrink, packed)
-                mean = lane < 2 * PW
+                block = jnp.where(
+                    lane < 2 * PW, both[0:PH, 0:width], both[PH : 2 * PH, 0:width]
+                )
+                ret_out[s, k] = block
+                ret_now[k] = block
+                spot = lax.rem(lane, 8 * K)
+                mean = spot < 0
                 for i, (f, c) in enumerate(EDGES):
                     if f < 2:
-                        mean = mean | (lane == 3 * PW + i)
-                both = jnp.where(mean, both[0:PH], both[PH : 2 * PH])
-                ret_out[s, k] = both
-                ret_now[k] = both
-                shifted = pltpu.roll(both, (8 * k - 3 * PW) % width, 1)
-                edge = jnp.where((lane >= 8 * k) & (lane < 8 * k + 8), shifted, edge)
+                        mean = mean | (spot == i)
+                side = jnp.where(mean, both[0:PH, width:], both[PH : 2 * PH, width:])
+                side = jnp.where(lane // (8 * K) == iota((PH, width), 0), side, 0.0)
+                edge = edge + pltpu.roll(side, 8 * k, 1)
 
             @pl.when(s < STEPS - 1)
             def _():
-                edge_out[s] = edge
-                send_to(1, tiles - 1, edge_out.at[s], edge_in.at[s, tile], edge_send.at[s], edge_recv.at[s])
+                edge_out[s, 0:1] = jnp.sum(edge, axis=0, keepdims=True)
+                send_to(
+                    1,
+                    tiles - 1,
+                    edge_out.at[s, pl.ds(0, 1)],
+                    edge_in.at[s, tile, pl.ds(0, 1)],
+                    edge_send.at[s],
+                    edge_recv.at[s],
+                )
 
             send_all(ret_out.at[s], ret_in.at[s, pl.ds(tile * K, K)], ret_send.at[s], ret_recv.at[s])
 
@@ -593,14 +625,18 @@
 
             @pl.when(s < STEPS - 1)
             def _():
+                owns = []
+                for k in range(K):
+                    ghosts[0, k] = ghosts[1, k]
+                    owns.append(dot(dot(grow, ret_now[k]), widen))
                 wait_all(ring_in.at[s], ring_recv.at[s])
                 ring_now[...] = ring_in[s]
-                wait_all(edge_in.at[s, pl.ds(0, tiles - 1)], edge_recv.at[s])
-                edge_now[...] = edge_in[s]
-                edge_now[tile] = edge
+                rings = [ring_terms(k) for k in range(K)]
+                wait_all(edge_in.at[s, pl.ds(0, tiles - 1), pl.ds(0, 1)], edge_recv.at[s])
+                edge_now[:, 0:1] = edge_in[s, :, 0:1]
+                edge_now[tile, 0:1] = edge_out[s, 0:1]
                 for k in range(K):
-                    ghosts[0, k] = ghosts[1, k]
-                    keep(ghosts.at[1], k, next_sides(k))
+                    keep(ghosts.at[1], k, next_sides(k, owns[k], rings[k]))
 
         for k in range(K):
             slot = pl.ds(k * FINE_ROWS, FINE_ROWS)
@@ -611,7 +647,7 @@
         for s in range(STEPS):
             wait_all(ret_in.at[s], ret_send.at[s])
         for s in range(STEPS - 1):
-            wait_all(edge_in.at[s, pl.ds(0, tiles - 1)], edge_send.at[s])
+            wait_all(edge_in.at[s, pl.ds(0, tiles - 1), pl.ds(0, 1)], edge_send.at[s])
 
 
 def on_device(n_row, n_nest, ocean_state, face_depth, face_open, nest_place, nest_host):

time: 43.4 us -> 41.7 us (0.961)
  Pallas kernels: 41.6 us -> 40 us
    pallas_call x1, Pallas kernels: 41.6 us -> 40 us  [on_device(): pl.pallas_call(functools.partial(kernel, n_row, n_nest), out_shape=jax.Sh...]
where the time goes in v3:
time: 41.7 us; the launch traced here: 41.5 us
  Pallas kernels  40 us (96%)
  local copies, waits for them, and re-layouts  1.54 us (4%)
    pallas_call x1, Pallas kernels, on_device(): pl.pallas_call(functools.partial(kernel, n_row, n_nest), out_shape=jax.Sh...  40 us
    unnamed x1, local copies, waits for them, and re-layouts  1.54 us

profile of v3, /device:TPU:0, one launch (start us, length us, event | category | flops | bytes accessed | tf_op | source)
XLA Modules:
  0.0 41.5 jit_solution(14885866075332389318)
XLA Ops:
  0.0 40.0 %shard_map.55 = f32[1,3,64,128]{3,2,1,0:T(8,128)} custom-call(s32[16]{0:T(128)} %place_ref.1, s32[16]{0:T(128)} %host_ref.1, f32[1,3,64,128]{3,2,1,0:T(8,128)} %state_ref.1, f32[1,2,64,128]{3,2,1,0:T(8,128)} %depth_ref.1, s32[1,2,64,128]{3,2,1,0:T(8,128)} %open_ref.1), custom_call_target="tpu_custom_call" | custom-call | tf_op jit(solution)/shard_map/pallas_call | solution.py:660
  40.0 1.5 %copy.7 = f32[1,3,64,128]{3,2,1,0:T(8,128)} copy(f32[1,3,64,128]{3,2,1,0:T(8,128)} %shard_map.55) | data formatting | bytes 196608

commit v4 on v3

--- a/solution.py
+++ b/solution.py
@@ -14,7 +14,6 @@
 STEPS = 4
 NPOS = K * (RR - 1)
 COURANT = 0.3
-HIGHEST = lax.Precision.HIGHEST
 MESH = pl.DeviceIdType.MESH
 FINE_ROWS = RR * PH
 TOP = (RR - 1) * PH // 2
@@ -47,8 +46,25 @@
     return east, south
 
 
-def dot(a, b):
-    return jnp.dot(a, b, precision=HIGHEST, preferred_element_type=jnp.float32)
+def parts(x):
+    high = x.astype(jnp.bfloat16).astype(jnp.float32)
+    rest = x - high
+    middle = rest.astype(jnp.bfloat16).astype(jnp.float32)
+    return high, middle, rest - middle
+
+
+def dot_by(x, chosen):
+    rows = x.shape[0]
+    stacked = jnp.concatenate(parts(x), axis=0).astype(jnp.bfloat16)
+    y = jnp.dot(stacked, chosen, preferred_element_type=jnp.float32)
+    return y[:rows] + (y[rows : 2 * rows] + y[2 * rows :])
+
+
+def dot_of(chosen, x):
+    cols = x.shape[1]
+    stacked = jnp.concatenate(parts(x), axis=1).astype(jnp.bfloat16)
+    y = jnp.dot(chosen, stacked, preferred_element_type=jnp.float32)
+    return y[:, :cols] + (y[:, cols : 2 * cols] + y[:, 2 * cols :])
 
 
 def pack_strips(tmp):
@@ -100,15 +116,33 @@
     return block
 
 
+def fold_column(field, column):
+    height, width = field.shape
+    lane = iota((8, width), 1)
+    block = jnp.zeros((8, width), jnp.float32)
+    for v in range(height // 8):
+        piece = pltpu.roll(field[8 * v : 8 * v + 8], (v - column) % width, 1)
+        block = jnp.where(lane == v, piece, block)
+    return block
+
+
+def unfold_column(block, height):
+    return jnp.concatenate([block[:, v : v + 1] for v in range(height // 8)], axis=0)
+
+
 def kernel(
     n_row,
     n_nest,
     place_ref,
     host_ref,
+    state_hbm,
+    depth_hbm,
+    open_hbm,
+    out_ref,
     state_ref,
     depth_ref,
     open_ref,
-    out_ref,
+    load_sems,
     st,
     tmp,
     first_out,
@@ -124,6 +158,7 @@
     east_out,
     south_out,
     level_out,
+    west_out,
     west_in,
     north_in,
     east_in,
@@ -166,6 +201,15 @@
             barrier, inc=1, device_id=(1 - sec, t // n_nest, lax.rem(t, n_nest)), device_id_type=MESH
         )
 
+    loads = [
+        pltpu.make_async_copy(source, target, load_sems.at[i])
+        for i, (source, target) in enumerate(
+            ((state_hbm, state_ref), (depth_hbm, depth_ref), (open_hbm, open_ref))
+        )
+    ]
+    for load in loads:
+        load.start()
+
     def send_to(section, count, src, dst, send_sem, recv_sem):
         @pl.loop(0, tiles)
         def _(i):
@@ -200,6 +244,8 @@
             def _():
                 pl.semaphore_signal(barrier, inc=1, device_id=device, device_id_type=MESH)
 
+        for load in loads:
+            load.wait()
         st[...] = state_ref[0]
         depth = [depth_ref[0, i] for i in range(2)]
         opened = [open_ref[0, i].astype(jnp.float32) for i in range(2)]
@@ -277,12 +323,12 @@
                 )
                 send_all(fixed_out, fixed_in.at[tile], fixed_sems.at[0], fixed_sems.at[1])
 
-            east_out[s] = eastward
+            east_out[s] = fold_column(eastward, width - 1)
             south_out[s] = southward[height - 8 :]
             to_east = halo(s, 0, east_out.at[s], west_in.at[s], east)
             to_south = halo(s, 1, south_out.at[s], north_in.at[s], south)
-            to_west = halo(s, 2, level_out.at[s], east_in.at[s], west)
-            to_north = halo(s, 3, level_out.at[s, pl.ds(0, 8)], south_in.at[s], north)
+            to_west = halo(s, 2, west_out.at[s], east_in.at[s], west)
+            to_north = halo(s, 3, level_out.at[s], south_in.at[s], north)
 
             @pl.when(has_east)
             def _():
@@ -304,10 +350,11 @@
                 surface,
                 eastward,
                 southward,
-                west_in[s][:, width - 1 : width],
+                unfold_column(west_in[s], height),
                 north_in[s][7:8, :],
             )
-            level_out[s] = level
+            level_out[s] = level[0:8]
+            west_out[s] = fold_column(level, 0)
 
             @pl.when(has_west)
             def _():
@@ -326,7 +373,7 @@
                 to_north.wait_recv()
 
             fluxes = new_fluxes(
-                eastward, southward, level, east_in[s][:, 0:1], south_in[s][0:1, :], depth, opened
+                eastward, southward, level, unfold_column(east_in[s], height), south_in[s][0:1, :], depth, opened
             )
             st[0] = level
             st[1] = fluxes[0]
@@ -367,11 +414,11 @@
 
             @pl.when(has_west)
             def _():
-                halo(s, 2, level_out.at[s], east_in.at[s], west).wait_send()
+                halo(s, 2, west_out.at[s], east_in.at[s], west).wait_send()
 
             @pl.when(has_north)
             def _():
-                halo(s, 3, level_out.at[s, pl.ds(0, 8)], south_in.at[s], north).wait_send()
+                halo(s, 3, level_out.at[s], south_in.at[s], north).wait_send()
 
         wait_all(first_in, first_sems.at[0])
         wait_all(fixed_in, fixed_sems.at[0])
@@ -387,7 +434,6 @@
                 barrier, inc=1, device_id=(sec, t // n_nest, lax.rem(t, n_nest)), device_id_type=MESH
             )
 
-        st[...] = state_ref[0]
         spots, lives = [], []
         for k in range(K):
             spot, live = jnp.int32(0), jnp.int32(0)
@@ -416,7 +462,7 @@
             source = iota((width, width), 0)
             fine = iota((width, width), 1)
             wanted = LEFT + columns[k] * PW + fine // RR
-            spread[k] = (source == wanted).astype(jnp.float32)
+            spread[k] = (source == wanted).astype(jnp.float32).astype(jnp.bfloat16)
         grow = (iota((FINE_ROWS, PH), 0) // RR == iota((FINE_ROWS, PH), 1)).astype(jnp.float32)
         gather_from = iota((3 * width, 2 * width), 0)
         gather_to = iota((3 * width, 2 * width), 1)
@@ -451,11 +497,15 @@
             jnp.where(shrink_from == (shrink_row - PH) * RR + RR - 1, 1.0, 0.0),
         )
 
+        grow, shrink, gather, fold, widen = [
+            m.astype(jnp.bfloat16) for m in (grow, shrink, gather, fold, widen)
+        ]
+
         def side_ghosts(block, k):
             lane, sub = iota((PH, width), 1), iota((PH, width), 0)
             tall_lane = iota((FINE_ROWS, width), 1)
-            tall = dot(grow, block)
-            wide = dot(block, spread[k])
+            tall = dot_of(grow, block)
+            wide = dot_by(block, spread[k])
             west_lane = bands[k] * (2 * (RR - 1)) + columns[k]
             west = jnp.sum(jnp.where(tall_lane == west_lane, tall, 0.0), axis=1, keepdims=True)
             east = jnp.sum(
@@ -491,7 +541,7 @@
 
         def ring_terms(k):
             ring = ring_now[homes[k]]
-            tall, wide = dot(grow, ring), dot(ring, spread[k])
+            tall, wide = dot_of(grow, ring), dot_by(ring, spread[k])
             base = bands[k] * (LEFT + (RR - 1) * PW) + 3 * columns[k]
             sides = [pick_lane(tall, base + i) for i in range(3)]
             lines = [pick_row(wide, 3 * bands[k] + i) for i in range(3)]
@@ -509,7 +559,7 @@
             for device, slot, cover in near[k]:
                 line = jnp.broadcast_to(edge_now[device, 0:1], (FINE_ROWS, width))
                 own_row = iota((FINE_ROWS, width), 1) // (8 * K) == iota((FINE_ROWS, width), 0) // RR
-                edges = dot(jnp.where(own_row, line, 0.0), fold)
+                edges = dot_by(jnp.where(own_row, line, 0.0), fold)
                 chosen = edges
                 for other in range(1, K):
                     chosen = jnp.where(
@@ -548,6 +598,9 @@
             rows = iota((FINE_ROWS, width), 0)
             return jnp.where(rows < RR, top, pltpu.roll(wide, RR, 0))[:, 0:1]
 
+        for load in loads:
+            load.wait()
+        st[...] = state_ref[0]
         pl.semaphore_wait(barrier, 2 * tiles - 1)
         wait_all(first_in, first_sems.at[1])
         for k in range(K):
@@ -575,8 +628,8 @@
                 st[0, slot] = surface
                 st[1, slot] = eastward
                 st[2, slot] = southward
-                packed = dot(jnp.concatenate([surface, eastward, southward], axis=1), gather)
-                both = dot(shrink, packed)
+                packed = dot_by(jnp.concatenate([surface, eastward, southward], axis=1), gather)
+                both = dot_of(shrink, packed)
                 block = jnp.where(
                     lane < 2 * PW, both[0:PH, 0:width], both[PH : 2 * PH, 0:width]
                 )
@@ -610,7 +663,7 @@
                 wait_all(fixed_in, fixed_sems.at[1])
                 for k in range(K):
                     fixed = fixed_in[homes[k]]
-                    tall, wide = dot(grow, fixed), dot(fixed, spread[k])
+                    tall, wide = dot_of(grow, fixed), dot_by(fixed, spread[k])
                     base = bands[k] * (LEFT + (RR - 1) * PW) + 3 * columns[k]
                     keep(
                         fixed_terms,
@@ -628,7 +681,7 @@
                 owns = []
                 for k in range(K):
                     ghosts[0, k] = ghosts[1, k]
-                    owns.append(dot(dot(grow, ret_now[k]), widen))
+                    owns.append(dot_by(dot_of(grow, ret_now[k]), widen))
                 wait_all(ring_in.at[s], ring_recv.at[s])
                 ring_now[...] = ring_in[s]
                 rings = [ring_terms(k) for k in range(K)]
@@ -655,14 +708,19 @@
     height, width = ocean_state.shape[2:]
     f32 = jnp.float32
     vmem = pl.BlockSpec(memory_space=pltpu.VMEM)
+    hbm = pl.BlockSpec(memory_space=pl.ANY)
     smem = pl.BlockSpec(memory_space=pltpu.SMEM)
     dma = pltpu.SemaphoreType.DMA
     return pl.pallas_call(
         functools.partial(kernel, n_row, n_nest),
         out_shape=jax.ShapeDtypeStruct(ocean_state.shape, f32),
-        in_specs=[smem, smem, vmem, vmem, vmem],
+        in_specs=[smem, smem, hbm, hbm, hbm],
         out_specs=vmem,
         scratch_shapes=[
+            pltpu.VMEM(ocean_state.shape, f32),
+            pltpu.VMEM(face_depth.shape, f32),
+            pltpu.VMEM(face_open.shape, jnp.int32),
+            dma((3,)),
             pltpu.VMEM((3, height, width), f32),
             pltpu.VMEM((6, height, width), f32),
             pltpu.VMEM((2, PH, width), f32),
@@ -675,14 +733,15 @@
             pltpu.VMEM((STEPS - 1, tiles, PH, width), f32),
             pltpu.VMEM((STEPS, K, PH, width), f32),
             pltpu.VMEM((STEPS, tiles * K, PH, width), f32),
-            pltpu.VMEM((STEPS, height, width), f32),
             pltpu.VMEM((STEPS, 8, width), f32),
-            pltpu.VMEM((STEPS, height, width), f32),
-            pltpu.VMEM((STEPS, height, width), f32),
             pltpu.VMEM((STEPS, 8, width), f32),
-            pltpu.VMEM((STEPS, height, width), f32),
             pltpu.VMEM((STEPS, 8, width), f32),
-            pltpu.VMEM((K, width, width), f32),
+            pltpu.VMEM((STEPS, 8, width), f32),
+            pltpu.VMEM((STEPS, 8, width), f32),
+            pltpu.VMEM((STEPS, 8, width), f32),
+            pltpu.VMEM((STEPS, 8, width), f32),
+            pltpu.VMEM((STEPS, 8, width), f32),
+            pltpu.VMEM((K, width, width), jnp.bfloat16),
             pltpu.VMEM((2, K, FINE_ROWS + 8, width), f32),
             pltpu.VMEM((tiles, PH, width), f32),
             pltpu.VMEM((tiles, PH, width), f32),

time: 41.7 us -> 40.2 us (0.964)
  Pallas kernels: 40 us -> 38.3 us
    pallas_call x1, Pallas kernels: 40 us -> 38.3 us  [on_device(): pl.pallas_call(functools.partial(kernel, n_row, n_nest), out_shape=jax.Sh...]
where the time goes in v4:
time: 40.2 us; the launch traced here: 39.8 us
  Pallas kernels  38.3 us (95%)
  local copies, waits for them, and re-layouts  1.54 us (4%)
    pallas_call x1, Pallas kernels, on_device(): pl.pallas_call(functools.partial(kernel, n_row, n_nest), out_shape=jax.Sh...  38.3 us
    unnamed x1, local copies, waits for them, and re-layouts  1.54 us

profile of v4, /device:TPU:0, one launch (start us, length us, event | category | flops | bytes accessed | tf_op | source)
XLA Modules:
  0.0 39.8 jit_solution(949882172870024978)
XLA Ops:
  0.0 38.3 %shard_map.55 = f32[1,3,64,128]{3,2,1,0:T(8,128)} custom-call(s32[16]{0:T(128)} %place_ref.1, s32[16]{0:T(128)} %host_ref.1, f32[1,3,64,128]{3,2,1,0:T(8,128)} %state_hbm.1, f32[1,2,64,128]{3,2,1,0:T(8,128)} %depth_hbm.1, s32[1,2,64,128]{3,2,1,0:T(8,128)} %open_hbm.1), custom_call_target="tpu_custom_call" | custom-call | tf_op jit(solution)/shard_map/pallas_call | solution.py:714
  38.3 1.5 %copy.7 = f32[1,3,64,128]{3,2,1,0:T(8,128)} copy(f32[1,3,64,128]{3,2,1,0:T(8,128)} %shard_map.55) | data formatting | bytes 196608

commit v5 on v4

--- a/solution.py
+++ b/solution.py
@@ -283,12 +283,28 @@
 
         @pl.loop(0, STEPS)
         def _(s):
-            surface, eastward, southward = st[0], st[1], st[2]
-            level = new_level(surface, eastward, southward, 0.0, 0.0)
-            fluxes = new_fluxes(eastward, southward, level, 0.0, 0.0, depth, opened)
-            tmp[0] = level
-            tmp[1] = fluxes[0]
-            tmp[2] = fluxes[1]
+            for band in range(K):
+                lo = band * FINE_ROWS + (TOP - 3) // 8 * 8
+                hi = band * FINE_ROWS + (TOP + PH + 3 + 7) // 8 * 8
+                old = [st[f, lo:hi] for f in range(3)]
+                level = new_level(old[0], old[1], old[2], 0.0, 0.0)
+                flux_e, flux_s = new_fluxes(
+                    old[1],
+                    old[2],
+                    level,
+                    0.0,
+                    0.0,
+                    [d[lo:hi] for d in depth],
+                    [o[lo:hi] for o in opened],
+                )
+                east_gap = flux_e - pltpu.roll(flux_e, 1, 1)
+                south_gap = flux_s - pltpu.roll(flux_s, 1, 0)
+                tmp[0, lo:hi] = level
+                tmp[1, lo:hi] = flux_e
+                tmp[2, lo:hi] = flux_s
+                tmp[3, lo:hi] = level - COURANT * (east_gap + south_gap)
+                tmp[4, lo:hi] = level - COURANT * (flux_e + south_gap)
+                tmp[5, lo:hi] = level - COURANT * (east_gap + flux_s)
 
             @pl.when(s == 0)
             def _():
@@ -302,13 +318,6 @@
 
             @pl.when(s < STEPS - 1)
             def _():
-                cols = iota((height, width), 1)
-                rows = iota((height, width), 0)
-                east_gap = fluxes[0] - jnp.where(cols == 0, 0.0, pltpu.roll(fluxes[0], 1, 1))
-                south_gap = fluxes[1] - jnp.where(rows == 0, 0.0, pltpu.roll(fluxes[1], 1, 0))
-                tmp[3] = level - COURANT * (east_gap + south_gap)
-                tmp[4] = level - COURANT * (fluxes[0] + south_gap)
-                tmp[5] = level - COURANT * (east_gap + fluxes[1])
                 ring_out[s] = pack_ring(
                     [(tmp, (3,), -1), (tmp, (1,), -1), (tmp, (4,), PW)],
                     [(tmp, (3,), -1), (tmp, (2,), -1), (tmp, (5,), PH)],
@@ -323,6 +332,7 @@
                 )
                 send_all(fixed_out, fixed_in.at[tile], fixed_sems.at[0], fixed_sems.at[1])
 
+            surface, eastward, southward = st[0], st[1], st[2]
             east_out[s] = fold_column(eastward, width - 1)
             south_out[s] = southward[height - 8 :]
             to_east = halo(s, 0, east_out.at[s], west_in.at[s], east)
@@ -611,25 +621,29 @@
         def _(s):
             edge = jnp.zeros((PH, width), jnp.float32)
             lane = iota((PH, width), 1)
-            for k in range(K):
-                slot = pl.ds(k * FINE_ROWS, FINE_ROWS)
-                old, new = kept(ghosts.at[0], k), kept(ghosts.at[1], k)
-                surface, eastward, southward = st[0, slot], st[1, slot], st[2, slot]
-                depth = [depth_ref[0, i, slot] for i in range(2)]
-                opened = [open_ref[0, i, slot].astype(jnp.float32) for i in range(2)]
-                for m in range(1, RR + 1):
+            slots = [pl.ds(k * FINE_ROWS, FINE_ROWS) for k in range(K)]
+            olds = [kept(ghosts.at[0], k) for k in range(K)]
+            news = [kept(ghosts.at[1], k) for k in range(K)]
+            fields = [[st[f, slot] for f in range(3)] for slot in slots]
+            depths = [[depth_ref[0, i, slot] for i in range(2)] for slot in slots]
+            opens = [[open_ref[0, i, slot].astype(jnp.float32) for i in range(2)] for slot in slots]
+            for m in range(1, RR + 1):
+                for k in range(K):
                     west_g, north_g, east_g, south_g = [
-                        a + (m / RR) * (b - a) for a, b in zip(old, new)
+                        a + (m / RR) * (b - a) for a, b in zip(olds[k], news[k])
                     ]
+                    surface, eastward, southward = fields[k]
                     surface = new_level(surface, eastward, southward, west_g, north_g)
                     eastward, southward = new_fluxes(
-                        eastward, southward, surface, east_g, south_g, depth, opened
+                        eastward, southward, surface, east_g, south_g, depths[k], opens[k]
                     )
-                st[0, slot] = surface
-                st[1, slot] = eastward
-                st[2, slot] = southward
-                packed = dot_by(jnp.concatenate([surface, eastward, southward], axis=1), gather)
-                both = dot_of(shrink, packed)
+                    fields[k] = [surface, eastward, southward]
+            sums = [dot_by(jnp.concatenate(fields[k], axis=1), gather) for k in range(K)]
+            sums = [dot_of(shrink, packed) for packed in sums]
+            for k in range(K):
+                for f in range(3):
+                    st[f, slots[k]] = fields[k][f]
+                both = sums[k]
                 block = jnp.where(
                     lane < 2 * PW, both[0:PH, 0:width], both[PH : 2 * PH, 0:width]
                 )
@@ -688,8 +702,9 @@
                 wait_all(edge_in.at[s, pl.ds(0, tiles - 1), pl.ds(0, 1)], edge_recv.at[s])
                 edge_now[:, 0:1] = edge_in[s, :, 0:1]
                 edge_now[tile, 0:1] = edge_out[s, 0:1]
+                sides = [next_sides(k, owns[k], rings[k]) for k in range(K)]
                 for k in range(K):
-                    keep(ghosts.at[1], k, next_sides(k, owns[k], rings[k]))
+                    keep(ghosts.at[1], k, sides[k])
 
         for k in range(K):
             slot = pl.ds(k * FINE_ROWS, FINE_ROWS)

time: 40.2 us -> 40 us (level)
  no operation moved by 1% of the time
where the time goes in v5:
time: 40 us; the launch traced here: 39.7 us
  Pallas kernels  38.1 us (95%)
  local copies, waits for them, and re-layouts  1.54 us (4%)
    pallas_call x1, Pallas kernels, on_device(): pl.pallas_call(functools.partial(kernel, n_row, n_nest), out_shape=jax.Sh...  38.1 us
    unnamed x1, local copies, waits for them, and re-layouts  1.54 us

profile of v5, /device:TPU:0, one launch (start us, length us, event | category | flops | bytes accessed | tf_op | source)
XLA Modules:
  0.0 39.7 jit_solution(5110627971342458455)
XLA Ops:
  0.0 38.1 %shard_map.55 = f32[1,3,64,128]{3,2,1,0:T(8,128)} custom-call(s32[16]{0:T(128)} %place_ref.1, s32[16]{0:T(128)} %host_ref.1, f32[1,3,64,128]{3,2,1,0:T(8,128)} %state_hbm.1, f32[1,2,64,128]{3,2,1,0:T(8,128)} %depth_hbm.1, s32[1,2,64,128]{3,2,1,0:T(8,128)} %open_hbm.1), custom_call_target="tpu_custom_call" | custom-call | tf_op jit(solution)/shard_map/pallas_call | solution.py:729
  38.1 1.5 %copy.7 = f32[1,3,64,128]{3,2,1,0:T(8,128)} copy(f32[1,3,64,128]{3,2,1,0:T(8,128)} %shard_map.55) | data formatting | bytes 196608
